TPU v7x, 32 devices: a whole 2x2x4 slice. The times are simulated.
32 devices in a mesh: rep: 8 (over y, x, core), tp: 4 (over z).
Axes of the slice: x: 2, y: 2, z: 4, core: 2. Of those that a mesh axis runs over, the one named last changes fastest.
Arguments:
- tokens_in: bfloat16 [16384, 8192], P('rep', 'tp'), may hold values from -6 to 6
- cotangent: bfloat16 [16384, 1024], P('rep', 'tp'), may hold values from -0.046875 to 0.046875
- master: float32 [4, 2048, 1024], P('tp', 'rep'), may hold values from -0.0625 to 0.0625
- moment_one: float32 [4, 2048, 1024], P('tp', 'rep'), may hold values from -4 to 4
- moment_two: float32 [4, 2048, 1024], P('tp', 'rep'), may hold values from 0.01 to 1
- inputs_one: bfloat16 [512, 8192], P('rep', 'tp'), may hold values from -6 to 6
- inputs_two: bfloat16 [512, 8192], P('rep', 'tp'), may hold values from -6 to 6
- queries_one: bfloat16 [512, 4096], P(('rep', 'tp')), may hold values from -128 to 128
- queries_two: bfloat16 [512, 4096], P(('rep', 'tp')), may hold values from -128 to 128
- cache_keys: bfloat16 [512, 128, 512], P(('rep', 'tp')), may hold values from -4 to 4
- cache_values: bfloat16 [512, 128, 512], P(('rep', 'tp')), may hold values from -6 to 6
- lengths: int32 [512], P(('rep', 'tp')), may hold values from 16 to 128
Outputs:
- master_new: float32 [4, 2048, 1024], P('tp', 'rep')
- moment_one_new: float32 [4, 2048, 1024], P('tp', 'rep')
- moment_two_new: float32 [4, 2048, 1024], P('tp', 'rep')
- projected_one: float32 [512, 1024], P(('rep', 'tp'))
- projected_two: float32 [512, 1024], P(('rep', 'tp'))
- attended_one: float32 [512, 4096], P(('rep', 'tp'))
- attended_two: float32 [512, 4096], P(('rep', 'tp'))
Inputs may be any that keep to these rules, and one draw needn't show every extreme that they name: The new key of step one takes position lengths and that of step two lengths + 1.
All inputs are finite; a program needn't handle non-finite values.
Results may differ from a plain program's by a relative error of at most 0.0029.
Values may be sent and summed in bfloat16 or wider, within the bound.
A program may use at most 64 MiB of HBM per device.

v0:
```python
import functools

import jax
import jax.numpy as jnp
from jax import lax
from jax.experimental import pallas as pl
from jax.experimental.pallas import tpu as pltpu
from jax.sharding import PartitionSpec as P

KVH = 4
QH = 32
HD = 128


learning_rate = 0.001
beta_one = 0.9
beta_two = 0.99
epsilon = 1e-08
weight_decay = 0.1
step_count = 10.0
rope_base = 500000.0


def rotate(vectors, positions):
    row_count = vectors.shape[0]
    half_size = HD // 2
    inverse = rope_base ** (-2.0 * jnp.arange(half_size).astype(jnp.float32) / HD)
    angles = positions.astype(jnp.float32)[:, None, None] * inverse[None, None, :]
    shaped = vectors.reshape(row_count, -1, HD)
    first_half = shaped[..., :half_size]
    second_half = shaped[..., half_size:]
    cosine = jnp.cos(angles)
    sine = jnp.sin(angles)
    turned = jnp.concatenate(
        [first_half * cosine - second_half * sine, second_half * cosine + first_half * sine],
        axis=-1,
    )
    return turned.reshape(row_count, -1)


def partial_scores(queries, all_keys, all_values, allowed):
    row_count = all_keys.shape[0]
    places = all_keys.shape[1]
    group_size = QH // KVH
    shaped_queries = queries.astype(jnp.float32).reshape(row_count, KVH, group_size, HD)
    shaped_keys = all_keys.astype(jnp.float32).reshape(row_count, places, KVH, HD)
    shaped_values = all_values.astype(jnp.float32).reshape(row_count, places, KVH, HD)
    scores = jnp.einsum("rkgd,rpkd->rkgp", shaped_queries, shaped_keys) / HD**0.5
    scores = jnp.where(allowed[:, None, None, :], scores, -1e30)
    highest = jnp.max(scores, axis=-1)
    weights = lax.optimization_barrier(
        jnp.exp(scores - highest[..., None]).astype(jnp.bfloat16)
    ).astype(jnp.float32)
    return (
        highest,
        jnp.sum(weights, axis=-1),
        jnp.einsum("rkgp,rpkd->rkgd", weights, shaped_values),
    )


def finish(highest, denominator, numerator):
    row_count = numerator.shape[0]
    return (numerator / denominator[..., None]).reshape(row_count, -1)


def combine(earlier, later):
    highest = jnp.maximum(earlier[0], later[0])
    scale_early = jnp.exp(earlier[0] - highest)
    scale_late = jnp.exp(later[0] - highest)
    denominator = earlier[1] * scale_early + later[1] * scale_late
    numerator = earlier[2] * scale_early[..., None] + later[2] * scale_late[..., None]
    return (highest, denominator, numerator)


MESH = pl.DeviceIdType.MESH
SUB = 128


def arrival_orders(n_tp, sub):
    orders = []
    for t in range(n_tp):
        pieces = []
        for b in range(n_tp):
            for u in range(sub):
                pieces.append((max(abs(b - t), 0) * sub + u + (sub if b == t else 0) * -1, abs(b - t), b, u))
        pieces.sort()
        orders.append([b * sub + u for _, _, b, u in pieces])
    return orders


def piece_at(orders, t, s):
    found = 0
    for place, order in enumerate(orders):
        for step, piece in enumerate(order):
            found = found + jnp.where(jnp.logical_and(t == place, s == step), piece, 0)
    return found


def sync_kernel(
    n_rep,
    n_tp,
    sub,
    tok_hbm,
    cot_hbm,
    master_hbm,
    m1_hbm,
    m2_hbm,
    keys_hbm,
    values_hbm,
    in1_ref,
    in2_ref,
    q1_ref,
    q2_ref,
    lengths_ref,
    master_out,
    m1_out,
    m2_out,
    p1_out,
    p2_out,
    att_out,
    state,
    keys,
    values,
    early_max,
    early_sum,
    early_mix,
    fresh,
    mask,
    table_ref,
    q_ref,
    state_sem,
    cache_sem,
    tok,
    cot,
    cot_t,
    a_send,
    a_keep,
    a_recv,
    b_send,
    b_recv,
    w_buf,
    part,
    part_recv,
    tok_sem,
    cot_sem,
    z_send_sem,
    z_recv_sem,
    a_sems,
    b_ss,
    b_rs,
    w_ss,
    w_rs,
    v_ss,
    v_rs,
    p_ss,
    p_rs,
):
    nc = n_rep // 2
    steps = n_tp * sub
    cw = SUB
    r = lax.axis_index("rep")
    t = lax.axis_index("tp")
    k = r // 2
    c = r % 2
    sibling = (2 * k + 1 - c, t)
    own_rows = master_hbm.shape[0]
    att_rows, groups, stacked, _ = q_ref.shape
    master_ref, m1_ref, m2_ref = state.at[0], state.at[1], state.at[2]
    load_state = [
        pltpu.make_async_copy(source, state.at[i], state_sem.at[i])
        for i, source in enumerate((master_hbm, m1_hbm, m2_hbm))
    ]
    load_cache = [
        pltpu.make_async_copy(keys_hbm, keys, cache_sem.at[0]),
        pltpu.make_async_copy(values_hbm, values, cache_sem.at[1]),
    ]
    orders = arrival_orders(n_tp, sub)

    def chip(j):
        return (k + j) % nc

    def source_chip(j):
        return (k + nc - j) % nc

    load_tok = pltpu.make_async_copy(tok_hbm, tok, tok_sem)
    load_cots = [
        pltpu.make_async_copy(
            cot_hbm.at[:, u * cw : (u + 1) * cw], cot.at[t * sub + u], cot_sem.at[u]
        )
        for u in range(sub)
    ]
    for load in load_cots:
        load.start()
    load_tok.start()

    barrier = pltpu.get_barrier_semaphore()
    pl.semaphore_signal(barrier, inc=1, device_id=sibling, device_id_type=MESH)
    for j in range(1, nc):
        pl.semaphore_signal(barrier, inc=1, device_id=(2 * chip(j) + c, t), device_id_type=MESH)
    for j in range(1, n_tp):
        pl.semaphore_signal(barrier, inc=1, device_id=(r, (t + j) % n_tp), device_id_type=MESH)
    pl.semaphore_wait(barrier, 1 + (nc - 1) + (n_tp - 1))

    half_tokens = tok_hbm.shape[0] // 2

    def z_copy(g, side, half):
        rows = pl.ds(half * half_tokens, half_tokens)
        target = jnp.minimum(t + 1, n_tp - 1) if side == 0 else jnp.maximum(t - 1, 0)
        return pltpu.make_async_remote_copy(
            cot.at[g, rows], cot.at[g, rows], z_send_sem.at[side, half, g], z_recv_sem.at[half, g],
            device_id=(r, target), device_id_type=MESH,
        )

    def z_goes(g, side):
        b = g // sub
        if side == 0:
            return jnp.logical_and(b <= t, t < n_tp - 1)
        return jnp.logical_and(b >= t, t > 0)

    def z_forward(g, half):
        for side in (0, 1):
            @pl.when(z_goes(g, side))
            def _():
                z_copy(g, side, half).start()

    for u, load in enumerate(load_cots):
        load.wait()
        for half in (0, 1):
            z_forward(t * sub + u, half)
    for load in load_cache + load_state:
        load.start()
    row_ids = lax.broadcasted_iota(jnp.int32, (att_rows, HD), 0)
    length = jnp.zeros((att_rows, HD), jnp.int32)
    for row in range(att_rows):
        length = jnp.where(row_ids == row, lengths_ref[row], length)
    table_ref[...] = decode_table(length[:, 0:1])
    for i, source in enumerate((q1_ref, q2_ref)):
        for h in range(groups):
            for place in range(stacked // 2):
                at = (h * (stacked // 2) + place) * HD
                q_ref[:, h, i * (stacked // 2) + place, :] = source[:, at : at + HD].astype(
                    jnp.float32
                )
    mask[...] = table_ref[:, 0:HD]
    load_tok.wait()
    for load in load_cache + load_state:
        load.wait()

    def a_copy(s):
        return pltpu.make_async_remote_copy(
            a_send.at[s], a_recv.at[s], a_sems.at[0, s], a_sems.at[1, s],
            device_id=sibling, device_id_type=MESH,
        )

    def b_copy(s, j):
        return pltpu.make_async_remote_copy(
            b_send.at[s, j - 1], b_recv.at[s, j - 1], b_ss.at[s, j - 1], b_rs.at[s, j - 1],
            device_id=(2 * chip(j) + c, t), device_id_type=MESH,
        )

    def w_copy(s, j):
        return pltpu.make_async_remote_copy(
            w_buf.at[s, r], w_buf.at[s, r], w_ss.at[s, j - 1], w_rs.at[s, j - 1],
            device_id=(2 * chip(j) + c, t), device_id_type=MESH,
        )

    def v_copy(s, j):
        row = 2 * source_chip(j) + c
        return pltpu.make_async_remote_copy(
            w_buf.at[s, row], w_buf.at[s, row], v_ss.at[s, j], v_rs.at[s, j],
            device_id=sibling, device_id_type=MESH,
        )

    def gradient_stage(s):
        g = piece_at(orders, t, s)

        def arrive(half):
            @pl.when(g // sub != t)
            def _():
                z_copy(g, 0, half).wait_recv()
                z_forward(g, half)

            rows = slice(half * half_tokens, (half + 1) * half_tokens)
            cot_t[...] = cot[g, rows].T

        def term(owner, half):
            at = pl.multiple_of(owner * own_rows, own_rows)
            rows = slice(half * half_tokens, (half + 1) * half_tokens)
            return jnp.dot(
                cot_t[...], tok[rows, pl.ds(at, own_rows)], preferred_element_type=jnp.float32
            )

        arrive(0)
        for q in range(nc):
            a_send[s, q] = term(2 * q + 1 - c, 0)
        for q in range(nc):
            a_keep[s, q] = term(2 * q + c, 0)
        arrive(1)
        for q in range(nc):
            a_send[s, q] = a_send[s, q] + term(2 * q + 1 - c, 1)
        a_copy(s).start()
        for q in range(nc):
            a_keep[s, q] = a_keep[s, q] + term(2 * q + c, 1)

    def chip_sum_stage(s):
        a_copy(s).wait_recv()
        for j in range(1, nc):
            q = chip(j)
            b_send[s, j - 1] = (a_keep[s, q] + a_recv[s, q]).astype(jnp.bfloat16)
            b_copy(s, j).start()

    def update_stage(s):
        total = a_keep[s, k] + a_recv[s, k]
        for j in range(1, nc):
            b_copy(s, j).wait_recv()
            total = total + b_recv[s, j - 1].astype(jnp.float32)
        gradient = total.T
        cols = pl.ds(pl.multiple_of(piece_at(orders, t, s) * cw, cw), cw)
        master = master_ref[:, cols]
        moment_one_new = beta_one * m1_ref[:, cols] + (1.0 - beta_one) * gradient
        moment_two_new = beta_two * m2_ref[:, cols] + (1.0 - beta_two) * gradient * gradient
        corrected_one = moment_one_new / (1.0 - beta_one**step_count)
        corrected_two = moment_two_new / (1.0 - beta_two**step_count)
        master_new = master - learning_rate * (
            corrected_one / (jnp.sqrt(corrected_two) + epsilon) + weight_decay * master
        )
        w_buf[s, r] = master_new.astype(jnp.bfloat16)
        for j in range(1, nc):
            w_copy(s, j).start()
        v_copy(s, 0).start()
        master_out[:, cols] = master_new
        m1_out[:, cols] = moment_one_new
        m2_out[:, cols] = moment_two_new

    def share_stage(s):
        for j in range(1, nc):
            w_copy(s, j).wait_recv()
            v_copy(s, j).start()

    at_end = jnp.logical_or(t == 0, t == n_tp - 1)

    def p_copy(g, j):
        to = (t + j) % n_tp
        return pltpu.make_async_remote_copy(
            part.at[g, to], part_recv.at[j - 1, g], p_ss.at[j - 1, g], p_rs.at[j - 1, g],
            device_id=(r, to), device_id_type=MESH,
        )

    def decode_stage(s):
        for j in range(nc):
            v_copy(s, j).wait_recv()
        g = piece_at(orders, t, s)
        block = w_buf[s].reshape(n_rep * own_rows, cw)
        for i, in_ref in enumerate((in1_ref, in2_ref)):
            product = jnp.dot(in_ref[...], block, preferred_element_type=jnp.float32)
            part[g, :, i] = product.reshape(n_tp, product.shape[0] // n_tp, cw)

        @pl.when(at_end)
        def _():
            for j in range(1, n_tp):
                p_copy(g, j).start()

    def cache_stage(s):
        per_step = att_rows // steps
        for i in range(per_step):
            row = s * per_step + i
            allowed = mask[pl.ds(row, 1), :] > 0.0
            for h in range(groups):
                head = slice(h * HD, (h + 1) * HD)
                scores = lax.dot_general(
                    q_ref[row, h].astype(jnp.bfloat16),
                    keys[row, :, head],
                    (((1,), (1,)), ((), ())),
                    preferred_element_type=jnp.float32,
                )
                scores = jnp.where(allowed, scores / HD**0.5, -1e30)
                highest = jnp.max(scores, axis=-1, keepdims=True)
                weights = jnp.exp(scores - highest).astype(jnp.bfloat16)
                total = jnp.sum(weights.astype(jnp.float32), axis=-1, keepdims=True)
                early_max[row, h] = jnp.broadcast_to(highest, (stacked, HD))
                early_sum[row, h] = jnp.broadcast_to(total, (stacked, HD))
                early_mix[row, h] = jnp.dot(
                    weights, values[row, :, head], preferred_element_type=jnp.float32
                )

    stages = (
        (chip_sum_stage, 1),
        (update_stage, 2),
        (share_stage, 3),
        (decode_stage, 4),
        (cache_stage, 0),
        (gradient_stage, 0),
    )

    @pl.loop(0, steps + 4)
    def _(it):
        for stage, lag in stages:
            @pl.when(jnp.logical_and(it >= lag, it < steps + lag))
            def _():
                stage(it - lag)

    @pl.when(jnp.logical_not(at_end))
    def _():
        @pl.loop(0, steps)
        def _(g):
            for j in range(1, n_tp):
                p_copy(g, j).start()

    @pl.loop(0, steps)
    def _(s):
        a_copy(s).wait_send()
        for j in range(1, nc):
            b_copy(s, j).wait_send()
            w_copy(s, j).wait_send()
        for j in range(nc):
            v_copy(s, j).wait_send()
        for side in (0, 1):
            @pl.when(z_goes(s, side))
            def _():
                z_copy(s, side, 0).wait_send()
                z_copy(s, side, 1).wait_send()

    for g in range(steps):
        for j in range(1, n_tp):
            p_copy(g, j).wait_recv()
        for i, out in enumerate((p1_out, p2_out)):
            total = part[g, t, i]
            for j in range(1, n_tp):
                total = total + part_recv[j - 1, g, i]
            out[:, g * cw : (g + 1) * cw] = total
    for i, out in enumerate((p1_out, p2_out)):
        total = out[...]
        cosine = table_ref[:, (1 + 2 * i) * HD : (2 + 2 * i) * HD]
        sine = table_ref[:, (2 + 2 * i) * HD : (3 + 2 * i) * HD]
        for h in range(groups):
            head = total[:, h * HD : (h + 1) * HD]
            turned = head * cosine + pltpu.roll(head, HD // 2, 1) * sine
            value = total[:, (groups + h) * HD : (groups + h + 1) * HD]
            fresh[i, h] = turned.astype(jnp.bfloat16).astype(jnp.float32)
            fresh[i, groups + h] = value.astype(jnp.bfloat16).astype(jnp.float32)

    second = lax.broadcasted_iota(jnp.int32, (stacked, 1), 0) >= stacked // 2
    unroll = 4 if att_rows % 4 == 0 else 1

    @pl.loop(0, att_rows // unroll)
    def _(block):
        for i in range(unroll):
            row = block * unroll + i
            for h in range(groups):
                query = q_ref[row, h]
                one = jnp.sum(query * fresh[0, h, pl.ds(row, 1), :], axis=-1, keepdims=True)
                two = jnp.sum(query * fresh[1, h, pl.ds(row, 1), :], axis=-1, keepdims=True)
                one = one / HD**0.5
                two = jnp.where(second, two / HD**0.5, -1e30)
                before = early_max[row, h]
                highest = jnp.maximum(before, jnp.maximum(one, two))
                scale = jnp.exp(before - highest)
                one = jnp.exp(one - highest).astype(jnp.bfloat16).astype(jnp.float32)
                two = jnp.exp(two - highest).astype(jnp.bfloat16).astype(jnp.float32)
                below = early_sum[row, h] * scale + one + two
                above = (
                    early_mix[row, h] * scale
                    + one * fresh[0, groups + h, pl.ds(row, 1), :]
                    + two * fresh[1, groups + h, pl.ds(row, 1), :]
                )
                att_out[row, h] = above / below

    @pl.loop(0, steps)
    def _(g):
        for j in range(1, n_tp):
            p_copy(g, j).wait_send()


def synchronise(
    n_rep,
    n_tp,
    tokens_in,
    cotangent,
    master,
    m1,
    m2,
    cache_keys,
    cache_values,
    inputs_one,
    inputs_two,
    queries_one,
    queries_two,
    lengths,
):
    tokens, width = tokens_in.shape
    sub = cotangent.shape[1] // SUB
    steps = n_tp * sub
    nc = n_rep // 2
    rows, cols = master.shape
    decode = inputs_one.shape[0]
    share = decode // n_tp
    f32, bf16 = jnp.float32, jnp.bfloat16
    stacked = (queries_one.shape[0], KVH, 2 * QH // KVH, HD)
    vmem = pl.BlockSpec(memory_space=pltpu.VMEM)
    hbm = pl.BlockSpec(memory_space=pl.ANY)
    dma = pltpu.SemaphoreType.DMA
    return pl.pallas_call(
        functools.partial(sync_kernel, n_rep, n_tp, sub),
        out_shape=[jax.ShapeDtypeStruct((rows, cols), f32)] * 3
        + [jax.ShapeDtypeStruct((share, cols), f32)] * 2
        + [jax.ShapeDtypeStruct(stacked, f32)],
        in_specs=[hbm] * 7 + [vmem] * 4 + [pl.BlockSpec(memory_space=pltpu.SMEM)],
        out_specs=[vmem] * 6,
        scratch_shapes=[
            pltpu.VMEM((3, rows, cols), f32),
            pltpu.VMEM(cache_keys.shape, bf16),
            pltpu.VMEM(cache_values.shape, bf16),
            pltpu.VMEM(stacked, f32),
            pltpu.VMEM(stacked, f32),
            pltpu.VMEM(stacked, f32),
            pltpu.VMEM((2, cols // HD, share, HD), f32),
            pltpu.VMEM((lengths.shape[0], HD), f32),
            pltpu.VMEM((lengths.shape[0], 5 * HD), f32),
            pltpu.VMEM(stacked, f32),
            dma((3,)),
            dma((2,)),
            pltpu.VMEM((tokens, width), bf16),
            pltpu.VMEM((steps, tokens, SUB), bf16),
            pltpu.VMEM((SUB, tokens // 2), bf16),
            pltpu.VMEM((steps, nc, SUB, rows), f32),
            pltpu.VMEM((steps, nc, SUB, rows), f32),
            pltpu.VMEM((steps, nc, SUB, rows), f32),
            pltpu.VMEM((steps, nc - 1, SUB, rows), bf16),
            pltpu.VMEM((steps, nc - 1, SUB, rows), bf16),
            pltpu.VMEM((steps, n_rep, rows, SUB), bf16),
            pltpu.VMEM((steps, n_tp, 2, share, SUB), f32),
            pltpu.VMEM((n_tp - 1, steps, 2, share, SUB), f32),
            dma(()),
            dma((sub,)),
            dma((2, 2, steps)),
            dma((2, steps)),
            dma((2, steps)),
            dma((steps, nc - 1)),
            dma((steps, nc - 1)),
            dma((steps, nc - 1)),
            dma((steps, nc - 1)),
            dma((steps, nc)),
            dma((steps, nc)),
            dma((n_tp - 1, steps)),
            dma((n_tp - 1, steps)),
        ],
        compiler_params=pltpu.CompilerParams(
            collective_id=0, has_side_effects=True, vmem_limit_bytes=58 * 2**20
        ),
        name="synchronise",
    )(
        tokens_in,
        cotangent,
        master,
        m1,
        m2,
        cache_keys,
        cache_values,
        inputs_one,
        inputs_two,
        queries_one,
        queries_two,
        lengths,
    )


def decode_table(lengths):
    shape = (lengths.shape[0], 5 * HD)
    column = lax.broadcasted_iota(jnp.int32, shape, 1)
    kind = column // HD
    lane = column % HD
    half_size = HD // 2
    inverse = rope_base ** (-2.0 * (lane % half_size).astype(jnp.float32) / HD)
    position = lengths + jnp.where(kind >= 3, 1, 0)
    angles = position.astype(jnp.float32) * inverse
    sine = jnp.where(lane < half_size, -jnp.sin(angles), jnp.sin(angles))
    allowed = jnp.where(lane < lengths, 1.0, 0.0)
    return jnp.where(kind == 0, allowed, jnp.where(kind % 2 == 1, jnp.cos(angles), sine))


def fits_kernel(n_rep, n_tp, cotangent, master, inputs_one, cache_keys):
    steps = n_tp * (cotangent.shape[1] // SUB)
    return (
        cache_keys.shape[1] == HD
        and steps > 0
        and cache_keys.shape[0] % max(steps, 1) == 0
        and n_rep % 2 == 0
        and n_rep >= 4
        and n_tp >= 2
        and cotangent.shape[1] % SUB == 0
        and cotangent.shape[0] % 256 == 0
        and master.shape[1] % 128 == 0
        and inputs_one.shape[0] % (8 * n_tp) == 0
    )


def shards(
    n_rep,
    n_tp,
    tokens_in,
    cotangent,
    master,
    moment_one,
    moment_two,
    inputs_one,
    inputs_two,
    queries_one,
    queries_two,
    cache_keys,
    cache_values,
    lengths,
):
    row_count = cache_keys.shape[0]
    if fits_kernel(n_rep, n_tp, cotangent, master[0], inputs_one, cache_keys):
        *updated, both_one, both_two, attended = synchronise(
            n_rep,
            n_tp,
            tokens_in,
            cotangent,
            master[0],
            moment_one[0],
            moment_two[0],
            cache_keys,
            cache_values,
            inputs_one,
            inputs_two,
            queries_one,
            queries_two,
            lengths,
        )
        half = QH // KVH
        return (
            *(array[None] for array in updated),
            both_one,
            both_two,
            attended[:, :, :half].reshape(row_count, -1),
            attended[:, :, half:].reshape(row_count, -1),
        )
    places = jnp.arange(cache_keys.shape[1], dtype=jnp.int32)
    cache_allowed = places[None, :] < lengths[:, None]
    fresh = jnp.zeros((row_count, 1), jnp.int32) == 0
    early_one = partial_scores(queries_one, cache_keys, cache_values, cache_allowed)
    early_two = partial_scores(queries_two, cache_keys, cache_values, cache_allowed)
    columns = lax.all_gather(cotangent, "tp", axis=1, tiled=True)
    gradient = lax.psum_scatter(
        lax.dot_general(
            tokens_in, columns, (((0,), (0,)), ((), ())), preferred_element_type=jnp.float32
        ),
        "rep",
        scatter_dimension=0,
        tiled=True,
    ).reshape(master.shape)
    moment_one_new = beta_one * moment_one + (1.0 - beta_one) * gradient
    moment_two_new = beta_two * moment_two + (1.0 - beta_two) * gradient * gradient
    corrected_one = moment_one_new / (1.0 - beta_one**step_count)
    corrected_two = moment_two_new / (1.0 - beta_two**step_count)
    master_new = master - learning_rate * (
        corrected_one / (jnp.sqrt(corrected_two) + epsilon) + weight_decay * master
    )
    weights = master_new[0].astype(jnp.bfloat16)
    shard_rows = lax.all_gather(weights, "rep", axis=0, tiled=True)
    partial_one = jnp.dot(inputs_one, shard_rows, preferred_element_type=jnp.float32)
    partial_two = jnp.dot(inputs_two, shard_rows, preferred_element_type=jnp.float32)
    both_one, both_two = (
        lax.psum_scatter(partial_one, "tp", scatter_dimension=0, tiled=True),
        lax.psum_scatter(partial_two, "tp", scatter_dimension=0, tiled=True),
    )
    key_width = both_one.shape[1] // 2
    keys_one = rotate(both_one[:, :key_width], lengths).astype(jnp.bfloat16)
    values_one = both_one[:, key_width:].astype(jnp.bfloat16)
    keys_two = rotate(both_two[:, :key_width], lengths + 1).astype(jnp.bfloat16)
    values_two = both_two[:, key_width:].astype(jnp.bfloat16)
    late_one = partial_scores(queries_one, keys_one[:, None], values_one[:, None], fresh)
    attended_one = finish(*combine(early_one, late_one))
    fresh_pair = jnp.concatenate([fresh, fresh], axis=1)
    late_two = partial_scores(
        queries_two,
        jnp.stack([keys_one, keys_two], axis=1),
        jnp.stack([values_one, values_two], axis=1),
        fresh_pair,
    )
    attended_two = finish(*combine(early_two, late_two))
    return (
        master_new,
        moment_one_new,
        moment_two_new,
        both_one,
        both_two,
        attended_one,
        attended_two,
    )


def solution(mesh):
    return jax.shard_map(
        functools.partial(shards, mesh.shape["rep"], mesh.shape["tp"]),
        mesh=mesh,
        in_specs=(
            P("rep", "tp"),
            P("rep", "tp"),
            P("tp", "rep", None),
            P("tp", "rep", None),
            P("tp", "rep", None),
            P("rep", "tp"),
            P("rep", "tp"),
            P(("rep", "tp"), None),
            P(("rep", "tp"), None),
            P(("rep", "tp"), None, None),
            P(("rep", "tp"), None, None),
            P(("rep", "tp")),
        ),
        out_specs=(
            P("tp", "rep", None),
            P("tp", "rep", None),
            P("tp", "rep", None),
            P(("rep", "tp"), None),
            P(("rep", "tp"), None),
            P(("rep", "tp"), None),
            P(("rep", "tp"), None),
        ),
        check_vma=False,
    )
```

profile of v0, /device:TPU:0, one launch (start us, length us, event | category | flops | bytes accessed | tf_op | source)
XLA Modules:
  0.0 111.3 jit_solution(7825958811660074416)
XLA Ops:
  0.6 104.2 %synchronise.1 = (f32[256,1024]{1,0:T(8,128)}, f32[256,1024]{1,0:T(8,128)}, f32[256,1024]{1,0:T(8,128)}, f32[16,1024]{1,0:T(8,128)}, f32[16,1024]{1,0:T(8,128)}, /*index=5*/f32[16,4,16,128]{3,2,1,0:T(8,128)}) custom-call(bf16[2048,2048]{1,0:T(8,128)(2,1)} %tok_hbm.1, bf16[2048,256]{1,0:T(8,128)(2,1)} %cot_hbm.1, f32[256,1024]{1,0:T(8,128)} %bitcast.14, ...), custom_call_target="tpu_custom_call" | custom-call | tf_op jit(solution)/shard_map/synchronise/pallas_call | solution.py:502
  104.8 0.0 copy-start.2
  104.8 0.0 copy-start.1
  104.8 1.2 %fusion = (f32[16,4,8,128]{3,2,1,0:T(8,128)S(1)}, f32[16,4,8,128]{3,2,1,0:T(8,128)S(1)}) fusion(f32[16,4,16,128]{3,2,1,0:T(8,128)} %get-tuple-element.18), kind=kLoop, calls=%fused_computation.2 | loop fusion | bytes 1048576 | tf_op jit(solution)/shard_map/slice | solution.py:637
  106.0 1.1 copy_bitcast_fusion
  107.1 0.0 copy-done.2
  107.1 0.0 copy-start
  107.1 1.0 copy.28
  108.1 0.0 copy-done.1
  108.1 0.0 copy-start.4
  108.1 0.0 copy-start.3
  108.1 1.0 copy.29
  109.1 0.0 copy-done
  109.1 1.0 copy.30
  110.1 0.0 copy-done.4
  110.1 0.6 copy.31
  110.7 0.0 copy-done.3
  110.7 0.6 copy.32
Async XLA Ops:
  104.8 2.3 %copy-start.2 = (f32[256,1024]{1,0:T(8,128)S(1)}, f32[256,1024]{1,0:T(8,128)}, u32[]{:S(2)}) copy-start(f32[256,1024]{1,0:T(8,128)} %get-tuple-element.13) | copy-start | bytes 3145732
  104.8 3.3 %copy-start.1 = (f32[256,1024]{1,0:T(8,128)S(1)}, f32[256,1024]{1,0:T(8,128)}, u32[]{:S(2)}) copy-start(f32[256,1024]{1,0:T(8,128)} %get-tuple-element.14) | copy-start | bytes 3145732
  107.1 2.0 %copy-start = (f32[256,1024]{1,0:T(8,128)S(1)}, f32[256,1024]{1,0:T(8,128)}, u32[]{:S(2)}) copy-start(f32[256,1024]{1,0:T(8,128)} %get-tuple-element.15) | copy-start | bytes 3145732
  108.1 1.9 %copy-start.4 = (f32[16,1024]{1,0:T(8,128)S(1)}, f32[16,1024]{1,0:T(8,128)}, u32[]{:S(2)}) copy-start(f32[16,1024]{1,0:T(8,128)} %get-tuple-element.33) | copy-start | bytes 196612
  108.1 2.6 %copy-start.3 = (f32[16,1024]{1,0:T(8,128)S(1)}, f32[16,1024]{1,0:T(8,128)}, u32[]{:S(2)}) copy-start(f32[16,1024]{1,0:T(8,128)} %get-tuple-element.34) | copy-start | bytes 196612
where the time goes:
time: 111 us
  Pallas kernels  104 us (94%)
  local copies, waits for them, and re-layouts  6.5 us (6%)
    pallas_call x1, Pallas kernels, synchronise(): pl.pallas_call(functools.partial(sync_kernel, n_rep, n_tp, sub), out_shap...  104 us
    unnamed x15, local copies, waits for them, and re-layouts  4.19 us

commit v1 on v0

--- a/solution.py
+++ b/solution.py
@@ -79,12 +79,17 @@
 def arrival_orders(n_tp, sub):
     orders = []
     for t in range(n_tp):
+        near = 0 if 2 * t < n_tp else n_tp - 1
+        inner = t not in (0, n_tp - 1)
         pieces = []
         for b in range(n_tp):
-            for u in range(sub):
-                pieces.append((max(abs(b - t), 0) * sub + u + (sub if b == t else 0) * -1, abs(b - t), b, u))
+            away = abs(b - t)
+            rank = away
+            if inner and away:
+                rank = 2 * away + (0 if (b > t) == (near == 0) else 1) - 1
+            pieces += [(rank, u, b) for u in range(sub)]
         pieces.sort()
-        orders.append([b * sub + u for _, _, b, u in pieces])
+        orders.append([b * sub + u for _, u, b in pieces])
     return orders
 
 
@@ -107,29 +112,31 @@
     m2_hbm,
     keys_hbm,
     values_hbm,
-    in1_ref,
-    in2_ref,
-    q1_ref,
-    q2_ref,
-    lengths_ref,
+    in1_hbm,
+    in2_hbm,
+    q1_hbm,
+    q2_hbm,
+    lengths_hbm,
     master_out,
     m1_out,
     m2_out,
     p1_out,
     p2_out,
-    att_out,
+    early_max,
+    early_sum,
+    early_mix,
+    table_ref,
+    queries,
     state,
     keys,
     values,
-    early_max,
-    early_sum,
-    early_mix,
-    fresh,
+    inputs,
+    lengths_ref,
     mask,
-    table_ref,
     q_ref,
     state_sem,
     cache_sem,
+    row_sem,
     tok,
     cot,
     cot_t,
@@ -174,6 +181,15 @@
         pltpu.make_async_copy(keys_hbm, keys, cache_sem.at[0]),
         pltpu.make_async_copy(values_hbm, values, cache_sem.at[1]),
     ]
+    load_rows = [
+        pltpu.make_async_copy(q1_hbm, queries.at[0], row_sem.at[0]),
+        pltpu.make_async_copy(q2_hbm, queries.at[1], row_sem.at[1]),
+        pltpu.make_async_copy(lengths_hbm, lengths_ref, row_sem.at[2]),
+    ]
+    load_inputs = [
+        pltpu.make_async_copy(in1_hbm, inputs.at[0], row_sem.at[3]),
+        pltpu.make_async_copy(in2_hbm, inputs.at[1], row_sem.at[4]),
+    ]
     orders = arrival_orders(n_tp, sub)
 
     def chip(j):
@@ -192,6 +208,8 @@
     for load in load_cots:
         load.start()
     load_tok.start()
+    for load in load_rows + load_cache + load_state + load_inputs:
+        load.start()
 
     barrier = pltpu.get_barrier_semaphore()
     pl.semaphore_signal(barrier, inc=1, device_id=sibling, device_id_type=MESH)
@@ -227,23 +245,23 @@
         load.wait()
         for half in (0, 1):
             z_forward(t * sub + u, half)
-    for load in load_cache + load_state:
-        load.start()
+    for load in load_rows:
+        load.wait()
     row_ids = lax.broadcasted_iota(jnp.int32, (att_rows, HD), 0)
     length = jnp.zeros((att_rows, HD), jnp.int32)
     for row in range(att_rows):
         length = jnp.where(row_ids == row, lengths_ref[row], length)
     table_ref[...] = decode_table(length[:, 0:1])
-    for i, source in enumerate((q1_ref, q2_ref)):
+    for i in range(2):
         for h in range(groups):
             for place in range(stacked // 2):
                 at = (h * (stacked // 2) + place) * HD
-                q_ref[:, h, i * (stacked // 2) + place, :] = source[:, at : at + HD].astype(
+                q_ref[:, h, i * (stacked // 2) + place, :] = queries[i, :, at : at + HD].astype(
                     jnp.float32
                 )
     mask[...] = table_ref[:, 0:HD]
     load_tok.wait()
-    for load in load_cache + load_state:
+    for load in load_cache + load_state + load_inputs:
         load.wait()
 
     def a_copy(s):
@@ -339,6 +357,10 @@
 
     at_end = jnp.logical_or(t == 0, t == n_tp - 1)
 
+    def to_end(j):
+        to = (t + j) % n_tp
+        return jnp.logical_or(to == 0, to == n_tp - 1)
+
     def p_copy(g, j):
         to = (t + j) % n_tp
         return pltpu.make_async_remote_copy(
@@ -351,13 +373,21 @@
             v_copy(s, j).wait_recv()
         g = piece_at(orders, t, s)
         block = w_buf[s].reshape(n_rep * own_rows, cw)
-        for i, in_ref in enumerate((in1_ref, in2_ref)):
-            product = jnp.dot(in_ref[...], block, preferred_element_type=jnp.float32)
+        for i in range(2):
+            product = jnp.dot(inputs[i], block, preferred_element_type=jnp.float32)
             part[g, :, i] = product.reshape(n_tp, product.shape[0] // n_tp, cw)
 
-        @pl.when(at_end)
-        def _():
-            for j in range(1, n_tp):
+        last = jnp.logical_and(at_end, s >= steps - 4)
+        for j in range(1, n_tp):
+            @pl.when(jnp.logical_or(last, jnp.logical_not(to_end(j))))
+            def _():
+                p_copy(g, j).start()
+
+    def late_stage(s):
+        g = piece_at(orders, t, s)
+        for j in range(1, n_tp):
+            @pl.when(to_end(j))
+            def _():
                 p_copy(g, j).start()
 
     def cache_stage(s):
@@ -377,11 +407,10 @@
                 highest = jnp.max(scores, axis=-1, keepdims=True)
                 weights = jnp.exp(scores - highest).astype(jnp.bfloat16)
                 total = jnp.sum(weights.astype(jnp.float32), axis=-1, keepdims=True)
-                early_max[row, h] = jnp.broadcast_to(highest, (stacked, HD))
-                early_sum[row, h] = jnp.broadcast_to(total, (stacked, HD))
-                early_mix[row, h] = jnp.dot(
-                    weights, values[row, :, head], preferred_element_type=jnp.float32
-                )
+                mix = jnp.dot(weights, values[row, :, head], preferred_element_type=jnp.float32)
+                for ref, value in ((early_max, highest), (early_sum, total), (early_mix, mix)):
+                    value = jnp.broadcast_to(value, (stacked, HD))
+                    ref[h, :, pl.ds(row, 1), :] = value.reshape(stacked, 1, HD)
 
     stages = (
         (chip_sum_stage, 1),
@@ -394,17 +423,30 @@
 
     @pl.loop(0, steps + 4)
     def _(it):
+        @pl.when(jnp.logical_and(at_end, it == steps))
+        def _():
+            @pl.loop(0, steps - 4)
+            def _(s):
+                late_stage(s)
+
         for stage, lag in stages:
             @pl.when(jnp.logical_and(it >= lag, it < steps + lag))
             def _():
                 stage(it - lag)
 
+    @pl.loop(0, steps)
+    def _(s):
+        for side in (0, 1):
+            @pl.when(z_goes(s, side))
+            def _():
+                z_copy(s, side, 0).wait_send()
+                z_copy(s, side, 1).wait_send()
+
     @pl.when(jnp.logical_not(at_end))
     def _():
         @pl.loop(0, steps)
-        def _(g):
-            for j in range(1, n_tp):
-                p_copy(g, j).start()
+        def _(s):
+            late_stage(s)
 
     @pl.loop(0, steps)
     def _(s):
@@ -414,11 +456,6 @@
             w_copy(s, j).wait_send()
         for j in range(nc):
             v_copy(s, j).wait_send()
-        for side in (0, 1):
-            @pl.when(z_goes(s, side))
-            def _():
-                z_copy(s, side, 0).wait_send()
-                z_copy(s, side, 1).wait_send()
 
     for g in range(steps):
         for j in range(1, n_tp):
@@ -428,47 +465,81 @@
             for j in range(1, n_tp):
                 total = total + part_recv[j - 1, g, i]
             out[:, g * cw : (g + 1) * cw] = total
-    for i, out in enumerate((p1_out, p2_out)):
-        total = out[...]
-        cosine = table_ref[:, (1 + 2 * i) * HD : (2 + 2 * i) * HD]
-        sine = table_ref[:, (2 + 2 * i) * HD : (3 + 2 * i) * HD]
+    @pl.loop(0, steps)
+    def _(g):
+        for j in range(1, n_tp):
+            p_copy(g, j).wait_send()
+
+
+def finish_kernel(
+    master,
+    m1,
+    m2,
+    p1,
+    p2,
+    early_max,
+    early_sum,
+    early_mix,
+    table,
+    queries,
+    master_out,
+    m1_out,
+    m2_out,
+    p1_out,
+    p2_out,
+    att1_out,
+    att2_out,
+    att,
+    sems,
+    att_sems,
+):
+    stores = [
+        pltpu.make_async_copy(source, target, sems.at[i])
+        for i, (source, target) in enumerate(
+            ((master, master_out), (m1, m1_out), (m2, m2_out), (p1, p1_out), (p2, p2_out))
+        )
+    ]
+    for store in stores:
+        store.start()
+    groups, stacked = early_max.shape[:2]
+    half = stacked // 2
+    keys, values = [], []
+    for i, ref in enumerate((p1, p2)):
+        total = ref[...]
+        cosine = table[:, (1 + 2 * i) * HD : (2 + 2 * i) * HD]
+        sine = table[:, (2 + 2 * i) * HD : (3 + 2 * i) * HD]
         for h in range(groups):
             head = total[:, h * HD : (h + 1) * HD]
             turned = head * cosine + pltpu.roll(head, HD // 2, 1) * sine
             value = total[:, (groups + h) * HD : (groups + h + 1) * HD]
-            fresh[i, h] = turned.astype(jnp.bfloat16).astype(jnp.float32)
-            fresh[i, groups + h] = value.astype(jnp.bfloat16).astype(jnp.float32)
-
-    second = lax.broadcasted_iota(jnp.int32, (stacked, 1), 0) >= stacked // 2
-    unroll = 4 if att_rows % 4 == 0 else 1
-
-    @pl.loop(0, att_rows // unroll)
-    def _(block):
-        for i in range(unroll):
-            row = block * unroll + i
-            for h in range(groups):
-                query = q_ref[row, h]
-                one = jnp.sum(query * fresh[0, h, pl.ds(row, 1), :], axis=-1, keepdims=True)
-                two = jnp.sum(query * fresh[1, h, pl.ds(row, 1), :], axis=-1, keepdims=True)
-                one = one / HD**0.5
-                two = jnp.where(second, two / HD**0.5, -1e30)
-                before = early_max[row, h]
-                highest = jnp.maximum(before, jnp.maximum(one, two))
+            keys.append(turned.astype(jnp.bfloat16).astype(jnp.float32))
+            values.append(value.astype(jnp.bfloat16).astype(jnp.float32))
+    for i, out in enumerate((att1_out, att2_out)):
+        for h in range(groups):
+            for place in range(half):
+                at = slice((h * half + place) * HD, (h * half + place + 1) * HD)
+                query = queries[i, :, at].astype(jnp.float32)
+                scores = [
+                    jnp.sum(query * keys[n * groups + h], axis=-1, keepdims=True) / HD**0.5
+                    for n in range(i + 1)
+                ]
+                before = early_max[h, i * half + place]
+                highest = before
+                for score in scores:
+                    highest = jnp.maximum(highest, score)
                 scale = jnp.exp(before - highest)
-                one = jnp.exp(one - highest).astype(jnp.bfloat16).astype(jnp.float32)
-                two = jnp.exp(two - highest).astype(jnp.bfloat16).astype(jnp.float32)
-                below = early_sum[row, h] * scale + one + two
-                above = (
-                    early_mix[row, h] * scale
-                    + one * fresh[0, groups + h, pl.ds(row, 1), :]
-                    + two * fresh[1, groups + h, pl.ds(row, 1), :]
-                )
-                att_out[row, h] = above / below
-
-    @pl.loop(0, steps)
-    def _(g):
-        for j in range(1, n_tp):
-            p_copy(g, j).wait_send()
+                below = early_sum[h, i * half + place] * scale
+                above = early_mix[h, i * half + place] * scale
+                for n, score in enumerate(scores):
+                    weight = jnp.exp(score - highest).astype(jnp.bfloat16).astype(jnp.float32)
+                    below = below + weight
+                    above = above + weight * values[n * groups + h]
+                att[i, :, at] = above / below
+        store = pltpu.make_async_copy(att.at[i], out, att_sems.at[i])
+        store.start()
+        stores.append(store)
+    for store in stores:
+        store.wait()
 
 
 def synchronise(
@@ -495,30 +566,31 @@
     decode = inputs_one.shape[0]
     share = decode // n_tp
     f32, bf16 = jnp.float32, jnp.bfloat16
-    stacked = (queries_one.shape[0], KVH, 2 * QH // KVH, HD)
+    count = queries_one.shape[0]
+    stacked = (count, KVH, 2 * QH // KVH, HD)
+    early = (KVH, 2 * QH // KVH, count, HD)
     vmem = pl.BlockSpec(memory_space=pltpu.VMEM)
     hbm = pl.BlockSpec(memory_space=pl.ANY)
     dma = pltpu.SemaphoreType.DMA
-    return pl.pallas_call(
+    held = pl.pallas_call(
         functools.partial(sync_kernel, n_rep, n_tp, sub),
-        out_shape=[jax.ShapeDtypeStruct((rows, cols), f32)] * 3
-        + [jax.ShapeDtypeStruct((share, cols), f32)] * 2
-        + [jax.ShapeDtypeStruct(stacked, f32)],
-        in_specs=[hbm] * 7 + [vmem] * 4 + [pl.BlockSpec(memory_space=pltpu.SMEM)],
-        out_specs=[vmem] * 6,
+        out_shape=[pltpu.VMEM((rows, cols), f32)] * 3
+        + [pltpu.VMEM((share, cols), f32)] * 2
+        + [pltpu.VMEM(early, f32)] * 3
+        + [pltpu.VMEM((count, 5 * HD), f32), pltpu.VMEM((2, *queries_one.shape), bf16)],
+        in_specs=[hbm] * 12,
+        out_specs=[vmem] * 10,
         scratch_shapes=[
             pltpu.VMEM((3, rows, cols), f32),
             pltpu.VMEM(cache_keys.shape, bf16),
             pltpu.VMEM(cache_values.shape, bf16),
-            pltpu.VMEM(stacked, f32),
-            pltpu.VMEM(stacked, f32),
-            pltpu.VMEM(stacked, f32),
-            pltpu.VMEM((2, cols // HD, share, HD), f32),
-            pltpu.VMEM((lengths.shape[0], HD), f32),
-            pltpu.VMEM((lengths.shape[0], 5 * HD), f32),
+            pltpu.VMEM((2, *inputs_one.shape), bf16),
+            pltpu.SMEM(lengths.shape, jnp.int32),
+            pltpu.VMEM((count, HD), f32),
             pltpu.VMEM(stacked, f32),
             dma((3,)),
             dma((2,)),
+            dma((5,)),
             pltpu.VMEM((tokens, width), bf16),
             pltpu.VMEM((steps, tokens, SUB), bf16),
             pltpu.VMEM((SUB, tokens // 2), bf16),
@@ -545,7 +617,7 @@
             dma((n_tp - 1, steps)),
         ],
         compiler_params=pltpu.CompilerParams(
-            collective_id=0, has_side_effects=True, vmem_limit_bytes=58 * 2**20
+            collective_id=0, has_side_effects=True, vmem_limit_bytes=52 * 2**20
         ),
         name="synchronise",
     )(
@@ -562,6 +634,18 @@
         queries_two,
         lengths,
     )
+    wide = queries_one.shape
+    return pl.pallas_call(
+        finish_kernel,
+        out_shape=[jax.ShapeDtypeStruct((rows, cols), f32)] * 3
+        + [jax.ShapeDtypeStruct((share, cols), f32)] * 2
+        + [jax.ShapeDtypeStruct(wide, f32)] * 2,
+        in_specs=[vmem] * 10,
+        out_specs=[hbm] * 7,
+        scratch_shapes=[pltpu.VMEM((2, *wide), f32), dma((5,)), dma((2,))],
+        compiler_params=pltpu.CompilerParams(vmem_limit_bytes=4 * 2**20),
+        name="finish",
+    )(*held)
 
 
 def decode_table(lengths):
@@ -612,7 +696,7 @@
 ):
     row_count = cache_keys.shape[0]
     if fits_kernel(n_rep, n_tp, cotangent, master[0], inputs_one, cache_keys):
-        *updated, both_one, both_two, attended = synchronise(
+        *updated, both_one, both_two, attended_one, attended_two = synchronise(
             n_rep,
             n_tp,
             tokens_in,
@@ -628,13 +712,12 @@
             queries_two,
             lengths,
         )
-        half = QH // KVH
         return (
             *(array[None] for array in updated),
             both_one,
             both_two,
-            attended[:, :, :half].reshape(row_count, -1),
-            attended[:, :, half:].reshape(row_count, -1),
+            attended_one,
+            attended_two,
         )
     places = jnp.arange(cache_keys.shape[1], dtype=jnp.int32)
     cache_allowed = places[None, :] < lengths[:, None]

time: 111 us -> 96.8 us (0.87)
  Pallas kernels: 104 us -> 96 us
  local copies, waits for them, and re-layouts: 6.5 us -> 0 us
    pallas_call x1, Pallas kernels: 104 us -> 94 us  [synchronise(): pl.pallas_call(functools.partial(sync_kernel, n_rep, n_tp, sub), out_shap...]
    unnamed x15 -> x0, local copies, waits for them, and re-layouts: 4.19 us -> none
    pallas_call x0 -> x1, Pallas kernels: none -> 1.93 us  [synchronise(): pl.pallas_call(finish_kernel, out_shape=[jax.ShapeDtypeStruct((rows, cols...]
    slice x1 -> x0, local copies, waits for them, and re-layouts: 1.21 us -> none  [shards(): attended[:, :, half:].reshape(row_count, -1)]
where the time goes in v1:
time: 96.8 us; the launch traced here: 96.6 us
  Pallas kernels  96 us (99%)
    pallas_call x1, Pallas kernels, synchronise(): pl.pallas_call(functools.partial(sync_kernel, n_rep, n_tp, sub), out_shap...  94 us

profile of v1, /device:TPU:0, one launch (start us, length us, event | category | flops | bytes accessed | tf_op | source)
XLA Modules:
  0.0 96.6 jit_solution(521927080294456248)
XLA Ops:
  0.6 94.0 %synchronise.1 = (f32[256,1024]{1,0:T(8,128)S(1)}, f32[256,1024]{1,0:T(8,128)S(1)}, f32[256,1024]{1,0:T(8,128)S(1)}, f32[16,1024]{1,0:T(8,128)S(1)}, f32[16,1024...) custom-call(bf16[2048,2048]{1,0:T(8,128)(2,1)} %tok_hbm.1, ...), custom_call_target="tpu_custom_call" | custom-call | tf_op jit(solution)/shard_map/synchronise/pallas_call | solution.py:575
  94.7 1.9 %finish.1 = (f32[256,1024]{1,0:T(8,128)}, f32[256,1024]{1,0:T(8,128)}, f32[256,1024]{1,0:T(8,128)}, f32[16,1024]{1,0:T(8,128)}, f32[16,1024]{1,0:T(8,128)}, /*index=5*/f32[16,4096]{1,0:T(8,128)}, f32[16,4096]{1,0:T(8,128)}) custom-call(f32[256,1024]{1,0:T(8,128)S(1)} %get-tuple-element.24.master, f32[256,1024]{1,0:T(8,128)S(1)} %get-tuple-element.25.m1, ...), custom_call_target="tpu_custom_call" | custom-call | tf_op jit(solution)/shard_map/finish/pallas_call | solution.py:638

commit v2 on v1

--- a/solution.py
+++ b/solution.py
@@ -74,6 +74,7 @@
 
 MESH = pl.DeviceIdType.MESH
 SUB = 128
+CHUNKS = (32, 32, 32, 32)
 
 
 def arrival_orders(n_tp, sub):
@@ -97,7 +98,11 @@
     found = 0
     for place, order in enumerate(orders):
         for step, piece in enumerate(order):
-            found = found + jnp.where(jnp.logical_and(t == place, s == step), piece, 0)
+            if isinstance(s, int):
+                if s == step:
+                    found = found + jnp.where(t == place, piece, 0)
+            else:
+                found = found + jnp.where(jnp.logical_and(t == place, s == step), piece, 0)
     return found
 
 
@@ -128,43 +133,45 @@
     table_ref,
     queries,
     state,
+    state_t,
+    new_t,
     keys,
     values,
     inputs,
     lengths_ref,
     mask,
     q_ref,
-    state_sem,
-    cache_sem,
-    row_sem,
     tok,
+    cot_raw,
     cot,
-    cot_t,
     a_send,
     a_keep,
     a_recv,
     b_send,
     b_recv,
     w_buf,
+    w_fine,
     part,
     part_recv,
-    tok_sem,
-    cot_sem,
-    z_send_sem,
-    z_recv_sem,
-    a_sems,
-    b_ss,
+    load_sem,
+    z_ss,
+    z_rs,
+    z_fs,
+    send_sem,
+    a_rs,
     b_rs,
-    w_ss,
     w_rs,
-    v_ss,
     v_rs,
-    p_ss,
     p_rs,
 ):
     nc = n_rep // 2
     steps = n_tp * sub
+    coarse = steps - 1
     cw = SUB
+    chunks = []
+    for width in CHUNKS:
+        chunks.append(slice(sum(CHUNKS[: len(chunks)]), sum(CHUNKS[: len(chunks)]) + width))
+    whole = slice(0, cw)
     r = lax.axis_index("rep")
     t = lax.axis_index("tp")
     k = r // 2
@@ -172,43 +179,42 @@
     sibling = (2 * k + 1 - c, t)
     own_rows = master_hbm.shape[0]
     att_rows, groups, stacked, _ = q_ref.shape
-    master_ref, m1_ref, m2_ref = state.at[0], state.at[1], state.at[2]
+    orders = arrival_orders(n_tp, sub)
+    last = piece_at(orders, t, coarse)
+    last_cols = pl.ds(pl.multiple_of(last * cw, cw), cw)
+
+    def chip(j):
+        return (k + j) % nc
+
+    def source_chip(j):
+        return (k + nc - j) % nc
+
+    def send(source, target, send_sem_ref, recv_sem_ref, device):
+        return pltpu.make_async_remote_copy(
+            source, target, send_sem_ref, recv_sem_ref, device_id=device, device_id_type=MESH
+        )
+
+    load_cot = pltpu.make_async_copy(cot_hbm, cot_raw, load_sem.at[0])
+    load_tok = pltpu.make_async_copy(tok_hbm, tok, load_sem.at[1])
+    load_lengths = pltpu.make_async_copy(lengths_hbm, lengths_ref, load_sem.at[2])
+    load_keys = pltpu.make_async_copy(keys_hbm, keys, load_sem.at[3])
+    load_values = pltpu.make_async_copy(values_hbm, values, load_sem.at[4])
+    load_queries = [
+        pltpu.make_async_copy(source, queries.at[i], load_sem.at[5 + i])
+        for i, source in enumerate((q1_hbm, q2_hbm))
+    ]
+    load_inputs = [
+        pltpu.make_async_copy(source, inputs.at[i], load_sem.at[7 + i])
+        for i, source in enumerate((in1_hbm, in2_hbm))
+    ]
     load_state = [
-        pltpu.make_async_copy(source, state.at[i], state_sem.at[i])
+        pltpu.make_async_copy(source, state.at[i], load_sem.at[9 + i])
         for i, source in enumerate((master_hbm, m1_hbm, m2_hbm))
     ]
-    load_cache = [
-        pltpu.make_async_copy(keys_hbm, keys, cache_sem.at[0]),
-        pltpu.make_async_copy(values_hbm, values, cache_sem.at[1]),
-    ]
-    load_rows = [
-        pltpu.make_async_copy(q1_hbm, queries.at[0], row_sem.at[0]),
-        pltpu.make_async_copy(q2_hbm, queries.at[1], row_sem.at[1]),
-        pltpu.make_async_copy(lengths_hbm, lengths_ref, row_sem.at[2]),
-    ]
-    load_inputs = [
-        pltpu.make_async_copy(in1_hbm, inputs.at[0], row_sem.at[3]),
-        pltpu.make_async_copy(in2_hbm, inputs.at[1], row_sem.at[4]),
-    ]
-    orders = arrival_orders(n_tp, sub)
-
-    def chip(j):
-        return (k + j) % nc
-
-    def source_chip(j):
-        return (k + nc - j) % nc
-
-    load_tok = pltpu.make_async_copy(tok_hbm, tok, tok_sem)
-    load_cots = [
-        pltpu.make_async_copy(
-            cot_hbm.at[:, u * cw : (u + 1) * cw], cot.at[t * sub + u], cot_sem.at[u]
-        )
-        for u in range(sub)
-    ]
-    for load in load_cots:
-        load.start()
+    load_cot.start()
     load_tok.start()
-    for load in load_rows + load_cache + load_state + load_inputs:
+    late_loads = [*load_queries, load_keys, load_values, *load_state, *load_inputs]
+    for load in [load_lengths, *late_loads]:
         load.start()
 
     barrier = pltpu.get_barrier_semaphore()
@@ -217,17 +223,20 @@
         pl.semaphore_signal(barrier, inc=1, device_id=(2 * chip(j) + c, t), device_id_type=MESH)
     for j in range(1, n_tp):
         pl.semaphore_signal(barrier, inc=1, device_id=(r, (t + j) % n_tp), device_id_type=MESH)
+    load_cot.wait()
+    for u in range(sub):
+        cot[t * sub + u] = cot_raw[:, u * cw : (u + 1) * cw].T
     pl.semaphore_wait(barrier, 1 + (nc - 1) + (n_tp - 1))
 
-    half_tokens = tok_hbm.shape[0] // 2
-
-    def z_copy(g, side, half):
-        rows = pl.ds(half * half_tokens, half_tokens)
-        target = jnp.minimum(t + 1, n_tp - 1) if side == 0 else jnp.maximum(t - 1, 0)
-        return pltpu.make_async_remote_copy(
-            cot.at[g, rows], cot.at[g, rows], z_send_sem.at[side, half, g], z_recv_sem.at[half, g],
-            device_id=(r, target), device_id_type=MESH,
-        )
+    def neighbour(side):
+        return jnp.minimum(t + 1, n_tp - 1) if side == 0 else jnp.maximum(t - 1, 0)
+
+    def z_copy(g, side):
+        return send(cot.at[g], cot.at[g], z_ss.at[side], z_rs.at[g], (r, neighbour(side)))
+
+    def z_chunk(g, side, f):
+        view = cot.at[g, chunks[f]]
+        return send(view, view, z_ss.at[side], z_fs.at[f], (r, neighbour(side)))
 
     def z_goes(g, side):
         b = g // sub
@@ -235,23 +244,44 @@
             return jnp.logical_and(b <= t, t < n_tp - 1)
         return jnp.logical_and(b >= t, t > 0)
 
-    def z_forward(g, half):
+    def in_chunks(g, side):
+        return g == piece_at(orders, neighbour(side), coarse)
+
+    def z_forward(g):
         for side in (0, 1):
-            @pl.when(z_goes(g, side))
+            @pl.when(jnp.logical_and(z_goes(g, side), jnp.logical_not(in_chunks(g, side))))
             def _():
-                z_copy(g, side, half).start()
-
-    for u, load in enumerate(load_cots):
-        load.wait()
-        for half in (0, 1):
-            z_forward(t * sub + u, half)
-    for load in load_rows:
-        load.wait()
+                z_copy(g, side).start()
+
+            @pl.when(jnp.logical_and(z_goes(g, side), in_chunks(g, side)))
+            def _():
+                for f in range(len(chunks)):
+                    z_chunk(g, side, f).start()
+
+    def z_forward_chunk(f):
+        for side in (0, 1):
+            @pl.when(jnp.logical_and(z_goes(last, side), in_chunks(last, side)))
+            def _():
+                z_chunk(last, side, f).start()
+
+            if f == len(chunks) - 1:
+                @pl.when(
+                    jnp.logical_and(z_goes(last, side), jnp.logical_not(in_chunks(last, side)))
+                )
+                def _():
+                    z_copy(last, side).start()
+
+    for u in range(sub):
+        z_forward(t * sub + u)
+    load_lengths.wait()
     row_ids = lax.broadcasted_iota(jnp.int32, (att_rows, HD), 0)
     length = jnp.zeros((att_rows, HD), jnp.int32)
     for row in range(att_rows):
         length = jnp.where(row_ids == row, lengths_ref[row], length)
     table_ref[...] = decode_table(length[:, 0:1])
+    mask[...] = table_ref[:, 0:HD]
+    for load in load_queries:
+        load.wait()
     for i in range(2):
         for h in range(groups):
             for place in range(stacked // 2):
@@ -259,101 +289,131 @@
                 q_ref[:, h, i * (stacked // 2) + place, :] = queries[i, :, at : at + HD].astype(
                     jnp.float32
                 )
-    mask[...] = table_ref[:, 0:HD]
     load_tok.wait()
-    for load in load_cache + load_state + load_inputs:
+    for load in late_loads[2:]:
         load.wait()
 
-    def a_copy(s):
-        return pltpu.make_async_remote_copy(
-            a_send.at[s], a_recv.at[s], a_sems.at[0, s], a_sems.at[1, s],
-            device_id=sibling, device_id_type=MESH,
+    def a_copy(s, cols, slot):
+        return send(
+            a_send.at[s, :, cols], a_recv.at[s, :, cols], send_sem.at[0], a_rs.at[slot], sibling
         )
 
-    def b_copy(s, j):
-        return pltpu.make_async_remote_copy(
-            b_send.at[s, j - 1], b_recv.at[s, j - 1], b_ss.at[s, j - 1], b_rs.at[s, j - 1],
-            device_id=(2 * chip(j) + c, t), device_id_type=MESH,
+    def b_copy(s, cols, slot, j):
+        return send(
+            b_send.at[s, j - 1, cols], b_recv.at[s, j - 1, cols], send_sem.at[1], b_rs.at[slot],
+            (2 * chip(j) + c, t),
         )
 
-    def w_copy(s, j):
-        return pltpu.make_async_remote_copy(
-            w_buf.at[s, r], w_buf.at[s, r], w_ss.at[s, j - 1], w_rs.at[s, j - 1],
-            device_id=(2 * chip(j) + c, t), device_id_type=MESH,
+    def w_at(s, cols, slot, row):
+        if isinstance(slot, int) and slot >= coarse:
+            return w_fine.at[row, cols]
+        return w_buf.at[s, row]
+
+    def w_send(slot):
+        return 2 if isinstance(slot, int) and slot >= coarse else 1
+
+    def w_copy(s, cols, slot, j):
+        view = w_at(s, cols, slot, r)
+        return send(
+            view, view, send_sem.at[1 + w_send(slot)], w_rs.at[slot], (2 * chip(j) + c, t)
         )
 
-    def v_copy(s, j):
-        row = 2 * source_chip(j) + c
-        return pltpu.make_async_remote_copy(
-            w_buf.at[s, row], w_buf.at[s, row], v_ss.at[s, j], v_rs.at[s, j],
-            device_id=sibling, device_id_type=MESH,
-        )
+    def v_copy(s, cols, slot, j):
+        view = w_at(s, cols, slot, 2 * source_chip(j) + c)
+        slot = coarse if w_send(slot) == 2 else slot
+        return send(view, view, send_sem.at[3 + w_send(slot)], v_rs.at[slot], sibling)
+
+    def wait_recv(ref, sem):
+        send(ref, ref, send_sem.at[0], sem, sibling).wait_recv()
+
+    def wait_send(ref, sem):
+        send(ref, ref, sem, a_rs.at[0], sibling).wait_send()
+
+    def terms(g, s, cols, slot):
+        def term(owner):
+            at = pl.multiple_of(owner * own_rows, own_rows)
+            return jnp.dot(
+                cot[g, cols], tok[:, pl.ds(at, own_rows)], preferred_element_type=jnp.float32
+            )
+
+        for q in range(nc):
+            a_send[s, q, cols] = term(2 * q + 1 - c)
+        a_copy(s, cols, slot).start()
+        for q in range(nc):
+            a_keep[s, q, cols] = term(2 * q + c)
 
     def gradient_stage(s):
         g = piece_at(orders, t, s)
 
-        def arrive(half):
-            @pl.when(g // sub != t)
-            def _():
-                z_copy(g, 0, half).wait_recv()
-                z_forward(g, half)
-
-            rows = slice(half * half_tokens, (half + 1) * half_tokens)
-            cot_t[...] = cot[g, rows].T
-
-        def term(owner, half):
-            at = pl.multiple_of(owner * own_rows, own_rows)
-            rows = slice(half * half_tokens, (half + 1) * half_tokens)
-            return jnp.dot(
-                cot_t[...], tok[rows, pl.ds(at, own_rows)], preferred_element_type=jnp.float32
-            )
-
-        arrive(0)
-        for q in range(nc):
-            a_send[s, q] = term(2 * q + 1 - c, 0)
-        for q in range(nc):
-            a_keep[s, q] = term(2 * q + c, 0)
-        arrive(1)
-        for q in range(nc):
-            a_send[s, q] = a_send[s, q] + term(2 * q + 1 - c, 1)
-        a_copy(s).start()
-        for q in range(nc):
-            a_keep[s, q] = a_keep[s, q] + term(2 * q + c, 1)
-
-    def chip_sum_stage(s):
-        a_copy(s).wait_recv()
+        @pl.when(g // sub != t)
+        def _():
+            z_copy(g, 0).wait_recv()
+            z_forward(g)
+
+        terms(g, s, whole, s)
+
+    def gradient_chunk(f):
+        z_chunk(last, 0, f).wait_recv()
+        z_forward_chunk(f)
+        terms(last, coarse, chunks[f], coarse + f)
+
+    def chip_sum_stage(s, cols, slot):
+        a_copy(s, cols, slot).wait_recv()
         for j in range(1, nc):
             q = chip(j)
-            b_send[s, j - 1] = (a_keep[s, q] + a_recv[s, q]).astype(jnp.bfloat16)
-            b_copy(s, j).start()
-
-    def update_stage(s):
-        total = a_keep[s, k] + a_recv[s, k]
+            b_send[s, j - 1, cols] = (a_keep[s, q, cols] + a_recv[s, q, cols]).astype(
+                jnp.bfloat16
+            )
+            b_copy(s, cols, slot, j).start()
+
+    def summed(s, cols, slot):
+        total = a_keep[s, k, cols] + a_recv[s, k, cols]
+        wait_recv(b_recv.at[s, :, cols], b_rs.at[slot])
         for j in range(1, nc):
-            b_copy(s, j).wait_recv()
-            total = total + b_recv[s, j - 1].astype(jnp.float32)
-        gradient = total.T
-        cols = pl.ds(pl.multiple_of(piece_at(orders, t, s) * cw, cw), cw)
-        master = master_ref[:, cols]
-        moment_one_new = beta_one * m1_ref[:, cols] + (1.0 - beta_one) * gradient
-        moment_two_new = beta_two * m2_ref[:, cols] + (1.0 - beta_two) * gradient * gradient
+            total = total + b_recv[s, j - 1, cols].astype(jnp.float32)
+        return total
+
+    def adam(master, m1, m2, gradient):
+        moment_one_new = beta_one * m1 + (1.0 - beta_one) * gradient
+        moment_two_new = beta_two * m2 + (1.0 - beta_two) * gradient * gradient
         corrected_one = moment_one_new / (1.0 - beta_one**step_count)
         corrected_two = moment_two_new / (1.0 - beta_two**step_count)
         master_new = master - learning_rate * (
             corrected_one / (jnp.sqrt(corrected_two) + epsilon) + weight_decay * master
         )
-        w_buf[s, r] = master_new.astype(jnp.bfloat16)
+        return master_new, moment_one_new, moment_two_new
+
+    outs = (master_out, m1_out, m2_out)
+
+    def spread(s, cols, slot):
         for j in range(1, nc):
-            w_copy(s, j).start()
-        v_copy(s, 0).start()
-        master_out[:, cols] = master_new
-        m1_out[:, cols] = moment_one_new
-        m2_out[:, cols] = moment_two_new
-
-    def share_stage(s):
+            w_copy(s, cols, slot, j).start()
+        v_copy(s, cols, slot, 0).start()
+
+    def update_stage(s):
+        cols = pl.ds(pl.multiple_of(piece_at(orders, t, s) * cw, cw), cw)
+        updated = adam(*(state[i, :, cols] for i in range(3)), summed(s, whole, s).T)
+        w_buf[s, r] = updated[0].astype(jnp.bfloat16)
+        spread(s, whole, s)
+        for out, value in zip(outs, updated):
+            out[:, cols] = value
+
+    def update_chunk(f):
+        cols = chunks[f]
+        updated = adam(*(state_t[i, cols] for i in range(3)), summed(coarse, cols, coarse + f))
+        w_fine[r, cols] = updated[0].astype(jnp.bfloat16)
+        spread(coarse, cols, coarse + f)
+        for i, value in enumerate(updated):
+            new_t[i, cols] = value
+
+    def share_stage(s, cols, slot):
+        if isinstance(slot, int) and slot >= coarse:
+            view = w_fine.at[0 : nc - 1, cols]
+        else:
+            view = w_buf.at[s, 0 : nc - 1]
+        wait_recv(view, w_rs.at[slot])
         for j in range(1, nc):
-            w_copy(s, j).wait_recv()
-            v_copy(s, j).start()
+            v_copy(s, cols, slot, j).start()
 
     at_end = jnp.logical_or(t == 0, t == n_tp - 1)
 
@@ -363,25 +423,54 @@
 
     def p_copy(g, j):
         to = (t + j) % n_tp
-        return pltpu.make_async_remote_copy(
-            part.at[g, to], part_recv.at[j - 1, g], p_ss.at[j - 1, g], p_rs.at[j - 1, g],
-            device_id=(r, to), device_id_type=MESH,
-        )
+        return send(part.at[g, to], part_recv.at[j - 1, g], send_sem.at[6], p_rs, (r, to))
+
+    def decoded(g, product):
+        rows = product.shape[0] // 2
+        for i in range(2):
+            part[g, :, i] = product[i * rows : (i + 1) * rows].reshape(n_tp, rows // n_tp, cw)
+
+    both = inputs.shape[0] * inputs.shape[1]
 
     def decode_stage(s):
-        for j in range(nc):
-            v_copy(s, j).wait_recv()
+        wait_recv(w_buf.at[s, 0:nc], v_rs.at[s])
         g = piece_at(orders, t, s)
         block = w_buf[s].reshape(n_rep * own_rows, cw)
-        for i in range(2):
-            product = jnp.dot(inputs[i], block, preferred_element_type=jnp.float32)
-            part[g, :, i] = product.reshape(n_tp, product.shape[0] // n_tp, cw)
-
-        last = jnp.logical_and(at_end, s >= steps - 4)
+        decoded(
+            g,
+            jnp.dot(
+                inputs[...].reshape(both, -1), block, preferred_element_type=jnp.float32
+            ),
+        )
         for j in range(1, n_tp):
-            @pl.when(jnp.logical_or(last, jnp.logical_not(to_end(j))))
+            @pl.when(jnp.logical_not(to_end(j)))
             def _():
                 p_copy(g, j).start()
+
+    def decode_last():
+        wait_recv(w_fine.at[0:nc], v_rs.at[coarse])
+        product = 0.0
+        for owner in range(n_rep):
+            rows = inputs[:, :, owner * own_rows : (owner + 1) * own_rows]
+            product = product + lax.dot_general(
+                rows.reshape(both, own_rows),
+                w_fine[owner],
+                (((1,), (1,)), ((), ())),
+                preferred_element_type=jnp.float32,
+            )
+        decoded(last, product)
+
+        @pl.when(at_end)
+        def _():
+            for j in range(1, n_tp):
+                p_copy(last, j).start()
+
+        @pl.when(jnp.logical_not(at_end))
+        def _():
+            for j in range(1, n_tp):
+                @pl.when(jnp.logical_not(to_end(j)))
+                def _():
+                    p_copy(last, j).start()
 
     def late_stage(s):
         g = piece_at(orders, t, s)
@@ -390,9 +479,13 @@
             def _():
                 p_copy(g, j).start()
 
+    cache_steps = min(4, coarse)
+
     def cache_stage(s):
-        per_step = att_rows // steps
-        for i in range(per_step):
+        per_step = att_rows // cache_steps
+
+        @pl.loop(0, per_step)
+        def _(i):
             row = s * per_step + i
             allowed = mask[pl.ds(row, 1), :] > 0.0
             for h in range(groups):
@@ -412,35 +505,74 @@
                     value = jnp.broadcast_to(value, (stacked, HD))
                     ref[h, :, pl.ds(row, 1), :] = value.reshape(stacked, 1, HD)
 
+    def turn_state():
+        for i in range(3):
+            state_t[i] = state[i, :, last_cols].T
+
     stages = (
-        (chip_sum_stage, 1),
-        (update_stage, 2),
-        (share_stage, 3),
-        (decode_stage, 4),
-        (cache_stage, 0),
-        (gradient_stage, 0),
+        (gradient_stage, 0, coarse),
+        (update_stage, 1, coarse),
+        (cache_stage, 0, cache_steps),
+        (lambda s: chip_sum_stage(s, whole, s), 0, coarse),
+        (lambda s: share_stage(s, whole, s), 2, coarse),
+        (decode_stage, 3, coarse),
     )
 
-    @pl.loop(0, steps + 4)
+    @pl.loop(0, coarse)
     def _(it):
-        @pl.when(jnp.logical_and(at_end, it == steps))
-        def _():
-            @pl.loop(0, steps - 4)
-            def _(s):
-                late_stage(s)
-
-        for stage, lag in stages:
-            @pl.when(jnp.logical_and(it >= lag, it < steps + lag))
+        for stage, lag, end in stages:
+            @pl.when(jnp.logical_and(it >= lag, it < end + lag))
             def _():
                 stage(it - lag)
 
-    @pl.loop(0, steps)
-    def _(s):
-        for side in (0, 1):
-            @pl.when(z_goes(s, side))
-            def _():
-                z_copy(s, side, 0).wait_send()
-                z_copy(s, side, 1).wait_send()
+        @pl.when(it == cache_steps - 1)
+        def _():
+            turn_state()
+
+    def update_any(n):
+        if n < coarse:
+            update_stage(n)
+        else:
+            update_chunk(n - coarse)
+
+    def share_any(n):
+        if n < coarse:
+            share_stage(n, whole, n)
+        else:
+            share_stage(coarse, chunks[n - coarse], n)
+
+    units = coarse + len(chunks)
+    for f, cols in enumerate(chunks):
+        n = coarse + f
+        gradient_chunk(f)
+        update_any(n - 1)
+        chip_sum_stage(coarse, cols, n)
+        share_any(n - 2)
+        if n - 3 < coarse:
+            decode_stage(n - 3)
+    for n in range(units - 3, coarse):
+        decode_stage(n)
+
+    @pl.when(at_end)
+    def _():
+        @pl.loop(0, coarse)
+        def _(s):
+            late_stage(s)
+
+    update_any(units - 1)
+    share_any(units - 2)
+    for out, value in zip(outs, (new_t.at[0], new_t.at[1], new_t.at[2])):
+        out[:, last_cols] = value[...].T
+    share_any(units - 1)
+    decode_last()
+
+    for place in range(n_tp):
+        @pl.when(t == place)
+        def _():
+            if place < n_tp - 1:
+                wait_send(cot.at[0 : (place + 1) * sub], z_ss.at[0])
+            if place > 0:
+                wait_send(cot.at[0 : (n_tp - place) * sub], z_ss.at[1])
 
     @pl.when(jnp.logical_not(at_end))
     def _():
@@ -448,27 +580,20 @@
         def _(s):
             late_stage(s)
 
-    @pl.loop(0, steps)
-    def _(s):
-        a_copy(s).wait_send()
-        for j in range(1, nc):
-            b_copy(s, j).wait_send()
-            w_copy(s, j).wait_send()
-        for j in range(nc):
-            v_copy(s, j).wait_send()
-
+    wait_send(a_send, send_sem.at[0])
+    wait_send(b_send, send_sem.at[1])
+    wait_send(w_buf.at[:, 0 : nc - 1], send_sem.at[2])
+    wait_send(w_fine.at[0 : nc - 1], send_sem.at[3])
+    wait_send(w_buf.at[:, 0:nc], send_sem.at[4])
+    wait_send(w_fine.at[0:nc], send_sem.at[5])
+    wait_recv(part_recv, p_rs)
     for g in range(steps):
-        for j in range(1, n_tp):
-            p_copy(g, j).wait_recv()
         for i, out in enumerate((p1_out, p2_out)):
             total = part[g, t, i]
             for j in range(1, n_tp):
                 total = total + part_recv[j - 1, g, i]
             out[:, g * cw : (g + 1) * cw] = total
-    @pl.loop(0, steps)
-    def _(g):
-        for j in range(1, n_tp):
-            p_copy(g, j).wait_send()
+    wait_send(part.at[:, 0 : n_tp - 1], send_sem.at[6])
 
 
 def finish_kernel(
@@ -561,6 +686,7 @@
     tokens, width = tokens_in.shape
     sub = cotangent.shape[1] // SUB
     steps = n_tp * sub
+    units = steps - 1 + len(CHUNKS)
     nc = n_rep // 2
     rows, cols = master.shape
     decode = inputs_one.shape[0]
@@ -582,39 +708,36 @@
         out_specs=[vmem] * 10,
         scratch_shapes=[
             pltpu.VMEM((3, rows, cols), f32),
+            pltpu.VMEM((3, SUB, rows), f32),
+            pltpu.VMEM((3, SUB, rows), f32),
             pltpu.VMEM(cache_keys.shape, bf16),
             pltpu.VMEM(cache_values.shape, bf16),
             pltpu.VMEM((2, *inputs_one.shape), bf16),
             pltpu.SMEM(lengths.shape, jnp.int32),
             pltpu.VMEM((count, HD), f32),
             pltpu.VMEM(stacked, f32),
-            dma((3,)),
-            dma((2,)),
-            dma((5,)),
             pltpu.VMEM((tokens, width), bf16),
-            pltpu.VMEM((steps, tokens, SUB), bf16),
-            pltpu.VMEM((SUB, tokens // 2), bf16),
+            pltpu.VMEM((tokens, sub * SUB), bf16),
+            pltpu.VMEM((steps, SUB, tokens), bf16),
             pltpu.VMEM((steps, nc, SUB, rows), f32),
             pltpu.VMEM((steps, nc, SUB, rows), f32),
             pltpu.VMEM((steps, nc, SUB, rows), f32),
             pltpu.VMEM((steps, nc - 1, SUB, rows), bf16),
             pltpu.VMEM((steps, nc - 1, SUB, rows), bf16),
-            pltpu.VMEM((steps, n_rep, rows, SUB), bf16),
+            pltpu.VMEM((steps - 1, n_rep, rows, SUB), bf16),
+            pltpu.VMEM((n_rep, SUB, rows), bf16),
             pltpu.VMEM((steps, n_tp, 2, share, SUB), f32),
             pltpu.VMEM((n_tp - 1, steps, 2, share, SUB), f32),
+            dma((12,)),
+            dma((2,)),
+            dma((steps,)),
+            dma((len(CHUNKS),)),
+            dma((7,)),
+            dma((units,)),
+            dma((units,)),
+            dma((units,)),
+            dma((steps,)),
             dma(()),
-            dma((sub,)),
-            dma((2, 2, steps)),
-            dma((2, steps)),
-            dma((2, steps)),
-            dma((steps, nc - 1)),
-            dma((steps, nc - 1)),
-            dma((steps, nc - 1)),
-            dma((steps, nc - 1)),
-            dma((steps, nc)),
-            dma((steps, nc)),
-            dma((n_tp - 1, steps)),
-            dma((n_tp - 1, steps)),
         ],
         compiler_params=pltpu.CompilerParams(
             collective_id=0, has_side_effects=True, vmem_limit_bytes=52 * 2**20
@@ -666,8 +789,8 @@
     steps = n_tp * (cotangent.shape[1] // SUB)
     return (
         cache_keys.shape[1] == HD
-        and steps > 0
-        and cache_keys.shape[0] % max(steps, 1) == 0
+        and steps > 4
+        and cache_keys.shape[0] % 4 == 0
         and n_rep % 2 == 0
         and n_rep >= 4
         and n_tp >= 2

time: 96.8 us -> 104 us (1.074)
  Pallas kernels: 96 us -> 103 us
    pallas_call x1, Pallas kernels: 94 us -> 101 us  [synchronise(): pl.pallas_call(functools.partial(sync_kernel, n_rep, n_tp, sub), out_shap...]
where the time goes in v2:
time: 104 us; the launch traced here: 103 us
  Pallas kernels  103 us (99%)
    pallas_call x1, Pallas kernels, synchronise(): pl.pallas_call(functools.partial(sync_kernel, n_rep, n_tp, sub), out_shap...  101 us

profile of v2, /device:TPU:0, one launch (start us, length us, event | category | flops | bytes accessed | tf_op | source)
XLA Modules:
  0.0 103.4 jit_solution(5945531253405666739)
XLA Ops:
  0.6 100.8 %synchronise.1 = (f32[256,1024]{1,0:T(8,128)S(1)}, f32[256,1024]{1,0:T(8,128)S(1)}, f32[256,1024]{1,0:T(8,128)S(1)}, f32[16,1024]{1,0:T(8,128)S(1)}, f32[16,1024...) custom-call(bf16[2048,2048]{1,0:T(8,128)(2,1)} %tok_hbm.1, ...), custom_call_target="tpu_custom_call" | custom-call | tf_op jit(solution)/shard_map/synchronise/pallas_call | solution.py:701
  101.5 1.9 %finish.1 = (f32[256,1024]{1,0:T(8,128)}, f32[256,1024]{1,0:T(8,128)}, f32[256,1024]{1,0:T(8,128)}, f32[16,1024]{1,0:T(8,128)}, f32[16,1024]{1,0:T(8,128)}, /*index=5*/f32[16,4096]{1,0:T(8,128)}, f32[16,4096]{1,0:T(8,128)}) custom-call(f32[256,1024]{1,0:T(8,128)S(1)} %get-tuple-element.24.master, f32[256,1024]{1,0:T(8,128)S(1)} %get-tuple-element.25.m1, ...), custom_call_target="tpu_custom_call" | custom-call | tf_op jit(solution)/shard_map/finish/pallas_call | solution.py:761

commit v3 on v2

--- a/solution.py
+++ b/solution.py
@@ -74,7 +74,7 @@
 
 MESH = pl.DeviceIdType.MESH
 SUB = 128
-CHUNKS = (32, 32, 32, 32)
+CHUNKS = (48, 32, 32, 16)
 
 
 def arrival_orders(n_tp, sub):
@@ -212,21 +212,17 @@
         for i, source in enumerate((master_hbm, m1_hbm, m2_hbm))
     ]
     load_cot.start()
-    load_tok.start()
-    late_loads = [*load_queries, load_keys, load_values, *load_state, *load_inputs]
-    for load in [load_lengths, *late_loads]:
-        load.start()
-
     barrier = pltpu.get_barrier_semaphore()
-    pl.semaphore_signal(barrier, inc=1, device_id=sibling, device_id_type=MESH)
-    for j in range(1, nc):
-        pl.semaphore_signal(barrier, inc=1, device_id=(2 * chip(j) + c, t), device_id_type=MESH)
+    for j in range(1, n_rep):
+        pl.semaphore_signal(barrier, inc=1, device_id=((r + j) % n_rep, t), device_id_type=MESH)
     for j in range(1, n_tp):
         pl.semaphore_signal(barrier, inc=1, device_id=(r, (t + j) % n_tp), device_id_type=MESH)
+    late_loads = [*load_queries, load_keys, load_values, *load_state, *load_inputs]
     load_cot.wait()
-    for u in range(sub):
-        cot[t * sub + u] = cot_raw[:, u * cw : (u + 1) * cw].T
-    pl.semaphore_wait(barrier, 1 + (nc - 1) + (n_tp - 1))
+    for load in [load_lengths, *late_loads[:4], load_tok, *late_loads[4:]]:
+        load.start()
+    cot[t * sub] = cot_raw[:, 0:cw].T
+    pl.semaphore_wait(barrier, (n_rep - 1) + (n_tp - 1))
 
     def neighbour(side):
         return jnp.minimum(t + 1, n_tp - 1) if side == 0 else jnp.maximum(t - 1, 0)
@@ -271,7 +267,9 @@
                 def _():
                     z_copy(last, side).start()
 
-    for u in range(sub):
+    z_forward(t * sub)
+    for u in range(1, sub):
+        cot[t * sub + u] = cot_raw[:, u * cw : (u + 1) * cw].T
         z_forward(t * sub + u)
     load_lengths.wait()
     row_ids = lax.broadcasted_iota(jnp.int32, (att_rows, HD), 0)
@@ -304,24 +302,27 @@
             (2 * chip(j) + c, t),
         )
 
-    def w_at(s, cols, slot, row):
-        if isinstance(slot, int) and slot >= coarse:
-            return w_fine.at[row, cols]
-        return w_buf.at[s, row]
-
-    def w_send(slot):
-        return 2 if isinstance(slot, int) and slot >= coarse else 1
-
-    def w_copy(s, cols, slot, j):
-        view = w_at(s, cols, slot, r)
+    def w_copy(s, j):
+        view = w_buf.at[s, r]
+        return send(view, view, send_sem.at[2], w_rs.at[s], (2 * chip(j) + c, t))
+
+    def w_chunk(f, j):
+        view = w_fine.at[r, chunks[f]]
+        return send(view, view, send_sem.at[3], w_rs.at[coarse + f], (2 * chip(j) + c, t))
+
+    def v_chunk(f, j):
+        view = w_fine.at[2 * source_chip(j) + c, chunks[f]]
+        return send(view, view, send_sem.at[6], v_rs.at[coarse], sibling)
+
+    def w_direct(j):
+        view = w_fine.at[r, chunks[-1]]
         return send(
-            view, view, send_sem.at[1 + w_send(slot)], w_rs.at[slot], (2 * chip(j) + c, t)
+            view, view, send_sem.at[7], w_rs.at[coarse + len(chunks) - 1], ((r + j) % n_rep, t)
         )
 
-    def v_copy(s, cols, slot, j):
-        view = w_at(s, cols, slot, 2 * source_chip(j) + c)
-        slot = coarse if w_send(slot) == 2 else slot
-        return send(view, view, send_sem.at[3 + w_send(slot)], v_rs.at[slot], sibling)
+    def v_copy(s, j):
+        view = w_buf.at[s, 2 * source_chip(j) + c]
+        return send(view, view, send_sem.at[4], v_rs.at[s], sibling)
 
     def wait_recv(ref, sem):
         send(ref, ref, send_sem.at[0], sem, sibling).wait_recv()
@@ -385,16 +386,13 @@
 
     outs = (master_out, m1_out, m2_out)
 
-    def spread(s, cols, slot):
-        for j in range(1, nc):
-            w_copy(s, cols, slot, j).start()
-        v_copy(s, cols, slot, 0).start()
-
     def update_stage(s):
         cols = pl.ds(pl.multiple_of(piece_at(orders, t, s) * cw, cw), cw)
         updated = adam(*(state[i, :, cols] for i in range(3)), summed(s, whole, s).T)
         w_buf[s, r] = updated[0].astype(jnp.bfloat16)
-        spread(s, whole, s)
+        for j in range(1, nc):
+            w_copy(s, j).start()
+        v_copy(s, 0).start()
         for out, value in zip(outs, updated):
             out[:, cols] = value
 
@@ -402,18 +400,25 @@
         cols = chunks[f]
         updated = adam(*(state_t[i, cols] for i in range(3)), summed(coarse, cols, coarse + f))
         w_fine[r, cols] = updated[0].astype(jnp.bfloat16)
-        spread(coarse, cols, coarse + f)
+        if f == len(chunks) - 1:
+            for j in range(1, n_rep):
+                w_direct(j).start()
+        else:
+            for j in range(1, nc):
+                w_chunk(f, j).start()
+            v_chunk(f, 0).start()
         for i, value in enumerate(updated):
             new_t[i, cols] = value
 
-    def share_stage(s, cols, slot):
-        if isinstance(slot, int) and slot >= coarse:
-            view = w_fine.at[0 : nc - 1, cols]
-        else:
-            view = w_buf.at[s, 0 : nc - 1]
-        wait_recv(view, w_rs.at[slot])
+    def share_stage(s):
+        wait_recv(w_buf.at[s, 0 : nc - 1], w_rs.at[s])
         for j in range(1, nc):
-            v_copy(s, cols, slot, j).start()
+            v_copy(s, j).start()
+
+    def share_chunk(f):
+        wait_recv(w_fine.at[0 : nc - 1, chunks[f]], w_rs.at[coarse + f])
+        for j in range(1, nc):
+            v_chunk(f, j).start()
 
     at_end = jnp.logical_or(t == 0, t == n_tp - 1)
 
@@ -423,7 +428,7 @@
 
     def p_copy(g, j):
         to = (t + j) % n_tp
-        return send(part.at[g, to], part_recv.at[j - 1, g], send_sem.at[6], p_rs, (r, to))
+        return send(part.at[g, to], part_recv.at[j - 1, g], send_sem.at[5], p_rs, (r, to))
 
     def decoded(g, product):
         rows = product.shape[0] // 2
@@ -448,7 +453,8 @@
                 p_copy(g, j).start()
 
     def decode_last():
-        wait_recv(w_fine.at[0:nc], v_rs.at[coarse])
+        wait_recv(w_fine.at[0 : n_rep - 1, chunks[-1]], w_rs.at[coarse + len(chunks) - 1])
+        wait_recv(w_fine.at[0:nc, 0 : chunks[-1].start], v_rs.at[coarse])
         product = 0.0
         for owner in range(n_rep):
             rows = inputs[:, :, owner * own_rows : (owner + 1) * own_rows]
@@ -509,49 +515,83 @@
         for i in range(3):
             state_t[i] = state[i, :, last_cols].T
 
+    def sum_stage(s):
+        chip_sum_stage(s, whole, s)
+
+    def ahead(s):
+        return jnp.logical_and(at_end, s >= cache_steps)
+
+    def never(s):
+        return False
+
     stages = (
-        (gradient_stage, 0, coarse),
-        (update_stage, 1, coarse),
-        (cache_stage, 0, cache_steps),
-        (lambda s: chip_sum_stage(s, whole, s), 0, coarse),
-        (lambda s: share_stage(s, whole, s), 2, coarse),
-        (decode_stage, 3, coarse),
+        (sum_stage, 1, ahead),
+        (update_stage, 2, lambda s: jnp.logical_and(at_end, s >= cache_steps - 1)),
+        (share_stage, 3, never),
+        (decode_stage, 4, never),
     )
+    cache_now = jnp.where(at_end, cache_steps, 1)
 
     @pl.loop(0, coarse)
     def _(it):
-        for stage, lag, end in stages:
-            @pl.when(jnp.logical_and(it >= lag, it < end + lag))
+        for stage, lag, skip in stages:
+            @pl.when(jnp.logical_and(it >= lag, jnp.logical_not(skip(it - lag))))
             def _():
                 stage(it - lag)
 
-        @pl.when(it == cache_steps - 1)
+        @pl.when(it < cache_now)
+        def _():
+            cache_stage(it)
+
+        gradient_stage(it)
+
+        @pl.when(jnp.logical_and(ahead(it), it < coarse - 1))
+        def _():
+            sum_stage(it)
+
+            @pl.when(it == cache_steps)
+            def _():
+                update_stage(it - 1)
+
+            update_stage(it)
+
+        @pl.when(it == cache_steps)
         def _():
             turn_state()
 
-    def update_any(n):
-        if n < coarse:
-            update_stage(n)
-        else:
-            update_chunk(n - coarse)
-
-    def share_any(n):
-        if n < coarse:
-            share_stage(n, whole, n)
-        else:
-            share_stage(coarse, chunks[n - coarse], n)
-
-    units = coarse + len(chunks)
+    sum_stage(coarse - 1)
+
+    @pl.when(jnp.logical_not(at_end))
+    def _():
+        update_stage(coarse - 2)
+
+    share_stage(coarse - 3)
+    decode_stage(coarse - 4)
+
+    @pl.when(jnp.logical_not(at_end))
+    def _():
+        cache_stage(1)
+
+    final = len(chunks) - 1
     for f, cols in enumerate(chunks):
-        n = coarse + f
         gradient_chunk(f)
-        update_any(n - 1)
-        chip_sum_stage(coarse, cols, n)
-        share_any(n - 2)
-        if n - 3 < coarse:
-            decode_stage(n - 3)
-    for n in range(units - 3, coarse):
-        decode_stage(n)
+        chip_sum_stage(coarse, cols, coarse + f)
+        if f == 0:
+            share_stage(coarse - 2)
+            if final > 1:
+                update_stage(coarse - 1)
+        if f > 1:
+            update_chunk(f - 2)
+    if final < 2:
+        update_stage(coarse - 1)
+    if final > 0:
+        update_chunk(final - 1)
+    update_chunk(final)
+    share_stage(coarse - 1)
+    for f in range(final - 1):
+        share_chunk(f)
+    for s in range(coarse - 3, coarse):
+        decode_stage(s)
 
     @pl.when(at_end)
     def _():
@@ -559,11 +599,10 @@
         def _(s):
             late_stage(s)
 
-    update_any(units - 1)
-    share_any(units - 2)
-    for out, value in zip(outs, (new_t.at[0], new_t.at[1], new_t.at[2])):
-        out[:, last_cols] = value[...].T
-    share_any(units - 1)
+    if final > 0:
+        share_chunk(final - 1)
+    for i, out in enumerate(outs):
+        out[:, last_cols] = new_t[i].T
     decode_last()
 
     for place in range(n_tp):
@@ -580,12 +619,17 @@
         def _(s):
             late_stage(s)
 
+        @pl.loop(2, cache_steps)
+        def _(s):
+            cache_stage(s)
+
     wait_send(a_send, send_sem.at[0])
     wait_send(b_send, send_sem.at[1])
     wait_send(w_buf.at[:, 0 : nc - 1], send_sem.at[2])
-    wait_send(w_fine.at[0 : nc - 1], send_sem.at[3])
+    wait_send(w_fine.at[0 : nc - 1, 0 : chunks[-1].start], send_sem.at[3])
+    wait_send(w_fine.at[0:nc, 0 : chunks[-1].start], send_sem.at[6])
+    wait_send(w_fine.at[0 : n_rep - 1, chunks[-1]], send_sem.at[7])
     wait_send(w_buf.at[:, 0:nc], send_sem.at[4])
-    wait_send(w_fine.at[0:nc], send_sem.at[5])
     wait_recv(part_recv, p_rs)
     for g in range(steps):
         for i, out in enumerate((p1_out, p2_out)):
@@ -593,7 +637,7 @@
             for j in range(1, n_tp):
                 total = total + part_recv[j - 1, g, i]
             out[:, g * cw : (g + 1) * cw] = total
-    wait_send(part.at[:, 0 : n_tp - 1], send_sem.at[6])
+    wait_send(part.at[:, 0 : n_tp - 1], send_sem.at[5])
 
 
 def finish_kernel(
@@ -732,7 +776,7 @@
             dma((2,)),
             dma((steps,)),
             dma((len(CHUNKS),)),
-            dma((7,)),
+            dma((8,)),
             dma((units,)),
             dma((units,)),
             dma((units,)),
@@ -789,7 +833,7 @@
     steps = n_tp * (cotangent.shape[1] // SUB)
     return (
         cache_keys.shape[1] == HD
-        and steps > 4
+        and steps > 6
         and cache_keys.shape[0] % 4 == 0
         and n_rep % 2 == 0
         and n_rep >= 4

time: 104 us -> 93 us (0.89)
  Pallas kernels: 103 us -> 92.2 us
    pallas_call x1, Pallas kernels: 101 us -> 90.2 us  [synchronise(): pl.pallas_call(functools.partial(sync_kernel, n_rep, n_tp, sub), out_shap...]
where the time goes in v3:
time: 93 us; the launch traced here: 92.8 us
  Pallas kernels  92.2 us (99%)
    pallas_call x1, Pallas kernels, synchronise(): pl.pallas_call(functools.partial(sync_kernel, n_rep, n_tp, sub), out_shap...  90.2 us
    pallas_call x1, Pallas kernels, synchronise(): pl.pallas_call(finish_kernel, out_shape=[jax.ShapeDtypeStruct((rows, cols...  1.93 us

profile of v3, /device:TPU:0, one launch (start us, length us, event | category | flops | bytes accessed | tf_op | source)
XLA Modules:
  0.0 92.8 jit_solution(11523525241928537179)
XLA Ops:
  0.6 90.2 %synchronise.1 = (f32[256,1024]{1,0:T(8,128)S(1)}, f32[256,1024]{1,0:T(8,128)S(1)}, f32[256,1024]{1,0:T(8,128)S(1)}, f32[16,1024]{1,0:T(8,128)S(1)}, f32[16,1024...) custom-call(bf16[2048,2048]{1,0:T(8,128)(2,1)} %tok_hbm.1, ...), custom_call_target="tpu_custom_call" | custom-call | tf_op jit(solution)/shard_map/synchronise/pallas_call | solution.py:745
  90.9 1.9 %finish.1 = (f32[256,1024]{1,0:T(8,128)}, f32[256,1024]{1,0:T(8,128)}, f32[256,1024]{1,0:T(8,128)}, f32[16,1024]{1,0:T(8,128)}, f32[16,1024]{1,0:T(8,128)}, /*index=5*/f32[16,4096]{1,0:T(8,128)}, f32[16,4096]{1,0:T(8,128)}) custom-call(f32[256,1024]{1,0:T(8,128)S(1)} %get-tuple-element.24.master, f32[256,1024]{1,0:T(8,128)S(1)} %get-tuple-element.25.m1, ...), custom_call_target="tpu_custom_call" | custom-call | tf_op jit(solution)/shard_map/finish/pallas_call | solution.py:805

commit v4 on v3

--- a/solution.py
+++ b/solution.py
@@ -468,8 +468,11 @@
 
         @pl.when(at_end)
         def _():
-            for j in range(1, n_tp):
-                p_copy(last, j).start()
+            for far in (True, False):
+                for j in range(1, n_tp):
+                    @pl.when(to_end(j) == far)
+                    def _():
+                        p_copy(last, j).start()
 
         @pl.when(jnp.logical_not(at_end))
         def _():
@@ -586,19 +589,27 @@
         update_stage(coarse - 1)
     if final > 0:
         update_chunk(final - 1)
-    update_chunk(final)
+    for s in range(coarse - 3, coarse - 1):
+        decode_stage(s)
     share_stage(coarse - 1)
-    for f in range(final - 1):
-        share_chunk(f)
-    for s in range(coarse - 3, coarse):
-        decode_stage(s)
 
     @pl.when(at_end)
     def _():
-        @pl.loop(0, coarse)
+        @pl.loop(0, coarse - 1)
         def _(s):
             late_stage(s)
 
+    for f in range(final - 2):
+        share_chunk(f)
+    decode_stage(coarse - 1)
+
+    @pl.when(at_end)
+    def _():
+        late_stage(coarse - 1)
+
+    update_chunk(final)
+    for f in range(max(final - 2, 0), final - 1):
+        share_chunk(f)
     if final > 0:
         share_chunk(final - 1)
     for i, out in enumerate(outs):
@@ -615,11 +626,13 @@
 
     @pl.when(jnp.logical_not(at_end))
     def _():
+        cache_stage(2)
+
         @pl.loop(0, steps)
         def _(s):
             late_stage(s)
 
-        @pl.loop(2, cache_steps)
+        @pl.loop(3, cache_steps)
         def _(s):
             cache_stage(s)
 

time: 93 us -> 91.6 us (0.985)
  Pallas kernels: 92.2 us -> 90.8 us
    pallas_call x1, Pallas kernels: 90.2 us -> 88.9 us  [synchronise(): pl.pallas_call(functools.partial(sync_kernel, n_rep, n_tp, sub), out_shap...]
where the time goes in v4:
time: 91.6 us; the launch traced here: 91.5 us
  Pallas kernels  90.8 us (99%)
    pallas_call x1, Pallas kernels, synchronise(): pl.pallas_call(functools.partial(sync_kernel, n_rep, n_tp, sub), out_shap...  88.9 us
    pallas_call x1, Pallas kernels, synchronise(): pl.pallas_call(finish_kernel, out_shape=[jax.ShapeDtypeStruct((rows, cols...  1.93 us

profile of v4, /device:TPU:0, one launch (start us, length us, event | category | flops | bytes accessed | tf_op | source)
XLA Modules:
  0.0 91.5 jit_solution(13216264316592653544)
XLA Ops:
  0.6 88.9 %synchronise.1 = (f32[256,1024]{1,0:T(8,128)S(1)}, f32[256,1024]{1,0:T(8,128)S(1)}, f32[256,1024]{1,0:T(8,128)S(1)}, f32[16,1024]{1,0:T(8,128)S(1)}, f32[16,1024...) custom-call(bf16[2048,2048]{1,0:T(8,128)(2,1)} %tok_hbm.1, ...), custom_call_target="tpu_custom_call" | custom-call | tf_op jit(solution)/shard_map/synchronise/pallas_call | solution.py:758
  89.5 1.9 %finish.1 = (f32[256,1024]{1,0:T(8,128)}, f32[256,1024]{1,0:T(8,128)}, f32[256,1024]{1,0:T(8,128)}, f32[16,1024]{1,0:T(8,128)}, f32[16,1024]{1,0:T(8,128)}, /*index=5*/f32[16,4096]{1,0:T(8,128)}, f32[16,4096]{1,0:T(8,128)}) custom-call(f32[256,1024]{1,0:T(8,128)S(1)} %get-tuple-element.24.master, f32[256,1024]{1,0:T(8,128)S(1)} %get-tuple-element.25.m1, ...), custom_call_target="tpu_custom_call" | custom-call | tf_op jit(solution)/shard_map/finish/pallas_call | solution.py:818

commit v5 on v4

--- a/solution.py
+++ b/solution.py
@@ -75,6 +75,7 @@
 MESH = pl.DeviceIdType.MESH
 SUB = 128
 CHUNKS = (48, 32, 32, 16)
+DIRECT = 2
 
 
 def arrival_orders(n_tp, sub):
@@ -151,6 +152,9 @@
     b_recv,
     w_buf,
     w_fine,
+    d_send,
+    d_recv,
+    d_own,
     part,
     part_recv,
     load_sem,
@@ -158,6 +162,7 @@
     z_rs,
     z_fs,
     send_sem,
+    d_rs,
     a_rs,
     b_rs,
     w_rs,
@@ -172,6 +177,11 @@
     for width in CHUNKS:
         chunks.append(slice(sum(CHUNKS[: len(chunks)]), sum(CHUNKS[: len(chunks)]) + width))
     whole = slice(0, cw)
+    final = len(chunks) - 1
+    direct = len(chunks) - DIRECT
+    shared_cols = slice(0, chunks[direct].start)
+    direct_cols = slice(chunks[direct].start, cw)
+    summed_cols = slice(0, chunks[final].start)
     r = lax.axis_index("rep")
     t = lax.axis_index("tp")
     k = r // 2
@@ -291,14 +301,20 @@
     for load in late_loads[2:]:
         load.wait()
 
+    def kind(slot, sem):
+        return send_sem.at[sem + (8 if isinstance(slot, int) and slot >= coarse else 0)]
+
+    def d_copy(at, owner, slot):
+        return send(d_send.at[at], d_recv.at[slot], send_sem.at[10], d_rs, (owner, t))
+
     def a_copy(s, cols, slot):
         return send(
-            a_send.at[s, :, cols], a_recv.at[s, :, cols], send_sem.at[0], a_rs.at[slot], sibling
+            a_send.at[s, :, cols], a_recv.at[s, :, cols], kind(slot, 0), a_rs.at[slot], sibling
         )
 
     def b_copy(s, cols, slot, j):
         return send(
-            b_send.at[s, j - 1, cols], b_recv.at[s, j - 1, cols], send_sem.at[1], b_rs.at[slot],
+            b_send.at[s, j - 1, cols], b_recv.at[s, j - 1, cols], kind(slot, 1), b_rs.at[slot],
             (2 * chip(j) + c, t),
         )
 
@@ -314,11 +330,9 @@
         view = w_fine.at[2 * source_chip(j) + c, chunks[f]]
         return send(view, view, send_sem.at[6], v_rs.at[coarse], sibling)
 
-    def w_direct(j):
-        view = w_fine.at[r, chunks[-1]]
-        return send(
-            view, view, send_sem.at[7], w_rs.at[coarse + len(chunks) - 1], ((r + j) % n_rep, t)
-        )
+    def w_direct(f, j):
+        view = w_fine.at[r, chunks[f]]
+        return send(view, view, send_sem.at[7], w_rs.at[coarse + f], ((r + j) % n_rep, t))
 
     def v_copy(s, j):
         view = w_buf.at[s, 2 * source_chip(j) + c]
@@ -357,6 +371,43 @@
         z_chunk(last, 0, f).wait_recv()
         z_forward_chunk(f)
         terms(last, coarse, chunks[f], coarse + f)
+
+    def gradient_final():
+        z_chunk(last, 0, final).wait_recv()
+        z_forward_chunk(final)
+
+        def term(owner):
+            at = pl.multiple_of(owner * own_rows, own_rows)
+            return jnp.dot(
+                cot[last, chunks[final]], tok[:, pl.ds(at, own_rows)],
+                preferred_element_type=jnp.float32,
+            )
+
+        goals = []
+        for i in range(nc - 1):
+            away = i + 1
+            if nc == 4:
+                away = (3 - 2 * (k % 2), 1 + k % 2, 2 + k % 2)[i]
+            for parity in range(2):
+                goals.append((2 * ((k + away) % nc) + parity, 2 * (away - 1) + c))
+        goals.append((2 * k + 1 - c, n_rep - 2))
+        group = 8
+        for start in range(0, n_rep, group):
+            now = range(start, min(start + group, n_rep - 1))
+            products = [term(goals[at][0]) for at in now]
+            if start + group >= n_rep:
+                d_own[...] = term(r)
+            for at, product in zip(now, products):
+                d_send[at] = product.astype(jnp.bfloat16)
+            for at in now:
+                d_copy(at, *goals[at]).start()
+
+    def summed_final():
+        total = d_own[...]
+        wait_recv(d_recv, d_rs)
+        for i in range(n_rep - 1):
+            total = total + d_recv[i].astype(jnp.float32)
+        return total
 
     def chip_sum_stage(s, cols, slot):
         a_copy(s, cols, slot).wait_recv()
@@ -398,11 +449,12 @@
 
     def update_chunk(f):
         cols = chunks[f]
-        updated = adam(*(state_t[i, cols] for i in range(3)), summed(coarse, cols, coarse + f))
+        total = summed_final() if f == final else summed(coarse, cols, coarse + f)
+        updated = adam(*(state_t[i, cols] for i in range(3)), total)
         w_fine[r, cols] = updated[0].astype(jnp.bfloat16)
-        if f == len(chunks) - 1:
+        if f >= direct:
             for j in range(1, n_rep):
-                w_direct(j).start()
+                w_direct(f, j).start()
         else:
             for j in range(1, nc):
                 w_chunk(f, j).start()
@@ -453,8 +505,9 @@
                 p_copy(g, j).start()
 
     def decode_last():
-        wait_recv(w_fine.at[0 : n_rep - 1, chunks[-1]], w_rs.at[coarse + len(chunks) - 1])
-        wait_recv(w_fine.at[0:nc, 0 : chunks[-1].start], v_rs.at[coarse])
+        for f in range(direct, final + 1):
+            wait_recv(w_fine.at[0 : n_rep - 1, chunks[f]], w_rs.at[coarse + f])
+        wait_recv(w_fine.at[0:nc, shared_cols], v_rs.at[coarse])
         product = 0.0
         for owner in range(n_rep):
             rows = inputs[:, :, owner * own_rows : (owner + 1) * own_rows]
@@ -575,20 +628,17 @@
     def _():
         cache_stage(1)
 
-    final = len(chunks) - 1
-    for f, cols in enumerate(chunks):
+    for f, cols in enumerate(chunks[:-1]):
         gradient_chunk(f)
         chip_sum_stage(coarse, cols, coarse + f)
         if f == 0:
             share_stage(coarse - 2)
-            if final > 1:
-                update_stage(coarse - 1)
+            update_stage(coarse - 1)
         if f > 1:
             update_chunk(f - 2)
-    if final < 2:
-        update_stage(coarse - 1)
-    if final > 0:
-        update_chunk(final - 1)
+    gradient_final()
+    if final > 1:
+        update_chunk(final - 2)
     for s in range(coarse - 3, coarse - 1):
         decode_stage(s)
     share_stage(coarse - 1)
@@ -599,19 +649,18 @@
         def _(s):
             late_stage(s)
 
-    for f in range(final - 2):
-        share_chunk(f)
+    update_chunk(final - 1)
+    update_chunk(final)
+    if direct > 0:
+        share_chunk(0)
     decode_stage(coarse - 1)
 
     @pl.when(at_end)
     def _():
         late_stage(coarse - 1)
 
-    update_chunk(final)
-    for f in range(max(final - 2, 0), final - 1):
+    for f in range(1, direct):
         share_chunk(f)
-    if final > 0:
-        share_chunk(final - 1)
     for i, out in enumerate(outs):
         out[:, last_cols] = new_t[i].T
     decode_last()
@@ -636,12 +685,15 @@
         def _(s):
             cache_stage(s)
 
-    wait_send(a_send, send_sem.at[0])
-    wait_send(b_send, send_sem.at[1])
+    wait_send(a_send.at[0:coarse], send_sem.at[0])
+    wait_send(b_send.at[0:coarse], send_sem.at[1])
+    wait_send(a_send.at[coarse, :, summed_cols], send_sem.at[8])
+    wait_send(b_send.at[coarse, :, summed_cols], send_sem.at[9])
+    wait_send(d_send, send_sem.at[10])
     wait_send(w_buf.at[:, 0 : nc - 1], send_sem.at[2])
-    wait_send(w_fine.at[0 : nc - 1, 0 : chunks[-1].start], send_sem.at[3])
-    wait_send(w_fine.at[0:nc, 0 : chunks[-1].start], send_sem.at[6])
-    wait_send(w_fine.at[0 : n_rep - 1, chunks[-1]], send_sem.at[7])
+    wait_send(w_fine.at[0 : nc - 1, shared_cols], send_sem.at[3])
+    wait_send(w_fine.at[0:nc, shared_cols], send_sem.at[6])
+    wait_send(w_fine.at[0 : n_rep - 1, direct_cols], send_sem.at[7])
     wait_send(w_buf.at[:, 0:nc], send_sem.at[4])
     wait_recv(part_recv, p_rs)
     for g in range(steps):
@@ -783,13 +835,17 @@
             pltpu.VMEM((steps, nc - 1, SUB, rows), bf16),
             pltpu.VMEM((steps - 1, n_rep, rows, SUB), bf16),
             pltpu.VMEM((n_rep, SUB, rows), bf16),
+            pltpu.VMEM((n_rep - 1, CHUNKS[-1], rows), bf16),
+            pltpu.VMEM((n_rep - 1, CHUNKS[-1], rows), bf16),
+            pltpu.VMEM((CHUNKS[-1], rows), f32),
             pltpu.VMEM((steps, n_tp, 2, share, SUB), f32),
             pltpu.VMEM((n_tp - 1, steps, 2, share, SUB), f32),
             dma((12,)),
             dma((2,)),
             dma((steps,)),
             dma((len(CHUNKS),)),
-            dma((8,)),
+            dma((11,)),
+            dma(()),
             dma((units,)),
             dma((units,)),
             dma((units,)),
@@ -847,6 +903,7 @@
     return (
         cache_keys.shape[1] == HD
         and steps > 6
+        and len(CHUNKS) > 2
         and cache_keys.shape[0] % 4 == 0
         and n_rep % 2 == 0
         and n_rep >= 4

time: 91.6 us -> 91 us (level)
  no operation moved by 1% of the time
where the time goes in v5:
time: 91 us; the launch traced here: 90.8 us
  Pallas kernels  90.2 us (99%)
    pallas_call x1, Pallas kernels, synchronise(): pl.pallas_call(functools.partial(sync_kernel, n_rep, n_tp, sub), out_shap...  88.3 us
    pallas_call x1, Pallas kernels, synchronise(): pl.pallas_call(finish_kernel, out_shape=[jax.ShapeDtypeStruct((rows, cols...  1.93 us

profile of v5, /device:TPU:0, one launch (start us, length us, event | category | flops | bytes accessed | tf_op | source)
XLA Modules:
  0.0 90.8 jit_solution(10751438292731800285)
XLA Ops:
  0.6 88.3 %synchronise.1 = (f32[256,1024]{1,0:T(8,128)S(1)}, f32[256,1024]{1,0:T(8,128)S(1)}, f32[256,1024]{1,0:T(8,128)S(1)}, f32[16,1024]{1,0:T(8,128)S(1)}, f32[16,1024...) custom-call(bf16[2048,2048]{1,0:T(8,128)(2,1)} %tok_hbm.1, ...), custom_call_target="tpu_custom_call" | custom-call | tf_op jit(solution)/shard_map/synchronise/pallas_call | solution.py:810
  88.9 1.9 %finish.1 = (f32[256,1024]{1,0:T(8,128)}, f32[256,1024]{1,0:T(8,128)}, f32[256,1024]{1,0:T(8,128)}, f32[16,1024]{1,0:T(8,128)}, f32[16,1024]{1,0:T(8,128)}, /*index=5*/f32[16,4096]{1,0:T(8,128)}, f32[16,4096]{1,0:T(8,128)}) custom-call(f32[256,1024]{1,0:T(8,128)S(1)} %get-tuple-element.24.master, f32[256,1024]{1,0:T(8,128)S(1)} %get-tuple-element.25.m1, ...), custom_call_target="tpu_custom_call" | custom-call | tf_op jit(solution)/shard_map/finish/pallas_call | solution.py:874

commit v6 on v5

--- a/solution.py
+++ b/solution.py
@@ -223,16 +223,25 @@
     ]
     load_cot.start()
     barrier = pltpu.get_barrier_semaphore()
-    for j in range(1, n_rep):
-        pl.semaphore_signal(barrier, inc=1, device_id=((r + j) % n_rep, t), device_id_type=MESH)
-    for j in range(1, n_tp):
-        pl.semaphore_signal(barrier, inc=1, device_id=(r, (t + j) % n_tp), device_id_type=MESH)
+    pl.semaphore_signal(barrier, inc=1, device_id=sibling, device_id_type=MESH)
+    for j in range(1, nc):
+        pl.semaphore_signal(barrier, inc=1, device_id=(2 * chip(j) + c, t), device_id_type=MESH)
+
+    @pl.when(t < n_tp - 1)
+    def _():
+        pl.semaphore_signal(barrier, inc=1, device_id=(r, t + 1), device_id_type=MESH)
+
+    @pl.when(t > 0)
+    def _():
+        pl.semaphore_signal(barrier, inc=1, device_id=(r, t - 1), device_id_type=MESH)
+
     late_loads = [*load_queries, load_keys, load_values, *load_state, *load_inputs]
     load_cot.wait()
     for load in [load_lengths, *late_loads[:4], load_tok, *late_loads[4:]]:
         load.start()
     cot[t * sub] = cot_raw[:, 0:cw].T
-    pl.semaphore_wait(barrier, (n_rep - 1) + (n_tp - 1))
+    near = jnp.where(t > 0, 1, 0) + jnp.where(t < n_tp - 1, 1, 0)
+    pl.semaphore_wait(barrier, nc + near)
 
     def neighbour(side):
         return jnp.minimum(t + 1, n_tp - 1) if side == 0 else jnp.maximum(t - 1, 0)

time: 91 us -> 90.6 us (level)
  no operation moved by 1% of the time
where the time goes in v6:
time: 90.6 us; the launch traced here: 90.4 us
  Pallas kernels  89.8 us (99%)
    pallas_call x1, Pallas kernels, synchronise(): pl.pallas_call(functools.partial(sync_kernel, n_rep, n_tp, sub), out_shap...  87.8 us
    pallas_call x1, Pallas kernels, synchronise(): pl.pallas_call(finish_kernel, out_shape=[jax.ShapeDtypeStruct((rows, cols...  1.93 us

profile of v6, /device:TPU:0, one launch (start us, length us, event | category | flops | bytes accessed | tf_op | source)
XLA Modules:
  0.0 90.4 jit_solution(8043056560482261594)
XLA Ops:
  0.6 87.8 %synchronise.1 = (f32[256,1024]{1,0:T(8,128)S(1)}, f32[256,1024]{1,0:T(8,128)S(1)}, f32[256,1024]{1,0:T(8,128)S(1)}, f32[16,1024]{1,0:T(8,128)S(1)}, f32[16,1024...) custom-call(bf16[2048,2048]{1,0:T(8,128)(2,1)} %tok_hbm.1, ...), custom_call_target="tpu_custom_call" | custom-call | tf_op jit(solution)/shard_map/synchronise/pallas_call | solution.py:819
  88.5 1.9 %finish.1 = (f32[256,1024]{1,0:T(8,128)}, f32[256,1024]{1,0:T(8,128)}, f32[256,1024]{1,0:T(8,128)}, f32[16,1024]{1,0:T(8,128)}, f32[16,1024]{1,0:T(8,128)}, /*index=5*/f32[16,4096]{1,0:T(8,128)}, f32[16,4096]{1,0:T(8,128)}) custom-call(f32[256,1024]{1,0:T(8,128)S(1)} %get-tuple-element.24.master, f32[256,1024]{1,0:T(8,128)S(1)} %get-tuple-element.25.m1, ...), custom_call_target="tpu_custom_call" | custom-call | tf_op jit(solution)/shard_map/finish/pallas_call | solution.py:883

commit v7 on v6

--- a/solution.py
+++ b/solution.py
@@ -76,6 +76,7 @@
 SUB = 128
 CHUNKS = (48, 32, 32, 16)
 DIRECT = 2
+RING = 4
 
 
 def arrival_orders(n_tp, sub):
@@ -310,6 +311,11 @@
     for load in late_loads[2:]:
         load.wait()
 
+    def ring(slot):
+        if isinstance(slot, int) and slot >= coarse:
+            return RING + slot - coarse
+        return slot % RING
+
     def kind(slot, sem):
         return send_sem.at[sem + (8 if isinstance(slot, int) and slot >= coarse else 0)]
 
@@ -318,22 +324,22 @@
 
     def a_copy(s, cols, slot):
         return send(
-            a_send.at[s, :, cols], a_recv.at[s, :, cols], kind(slot, 0), a_rs.at[slot], sibling
+            a_send.at[s, :, cols], a_recv.at[s, :, cols], kind(slot, 0), a_rs.at[ring(slot)], sibling
         )
 
     def b_copy(s, cols, slot, j):
         return send(
-            b_send.at[s, j - 1, cols], b_recv.at[s, j - 1, cols], kind(slot, 1), b_rs.at[slot],
+            b_send.at[s, j - 1, cols], b_recv.at[s, j - 1, cols], kind(slot, 1), b_rs.at[ring(slot)],
             (2 * chip(j) + c, t),
         )
 
     def w_copy(s, j):
         view = w_buf.at[s, r]
-        return send(view, view, send_sem.at[2], w_rs.at[s], (2 * chip(j) + c, t))
+        return send(view, view, send_sem.at[2], w_rs.at[ring(s)], (2 * chip(j) + c, t))
 
     def w_chunk(f, j):
         view = w_fine.at[r, chunks[f]]
-        return send(view, view, send_sem.at[3], w_rs.at[coarse + f], (2 * chip(j) + c, t))
+        return send(view, view, send_sem.at[3], w_rs.at[ring(coarse + f)], (2 * chip(j) + c, t))
 
     def v_chunk(f, j):
         view = w_fine.at[2 * source_chip(j) + c, chunks[f]]
@@ -341,7 +347,7 @@
 
     def w_direct(f, j):
         view = w_fine.at[r, chunks[f]]
-        return send(view, view, send_sem.at[7], w_rs.at[coarse + f], ((r + j) % n_rep, t))
+        return send(view, view, send_sem.at[7], w_rs.at[ring(coarse + f)], ((r + j) % n_rep, t))
 
     def v_copy(s, j):
         view = w_buf.at[s, 2 * source_chip(j) + c]
@@ -429,7 +435,7 @@
 
     def summed(s, cols, slot):
         total = a_keep[s, k, cols] + a_recv[s, k, cols]
-        wait_recv(b_recv.at[s, :, cols], b_rs.at[slot])
+        wait_recv(b_recv.at[s, :, cols], b_rs.at[ring(slot)])
         for j in range(1, nc):
             total = total + b_recv[s, j - 1, cols].astype(jnp.float32)
         return total
@@ -472,12 +478,12 @@
             new_t[i, cols] = value
 
     def share_stage(s):
-        wait_recv(w_buf.at[s, 0 : nc - 1], w_rs.at[s])
+        wait_recv(w_buf.at[s, 0 : nc - 1], w_rs.at[ring(s)])
         for j in range(1, nc):
             v_copy(s, j).start()
 
     def share_chunk(f):
-        wait_recv(w_fine.at[0 : nc - 1, chunks[f]], w_rs.at[coarse + f])
+        wait_recv(w_fine.at[0 : nc - 1, chunks[f]], w_rs.at[ring(coarse + f)])
         for j in range(1, nc):
             v_chunk(f, j).start()
 
@@ -515,7 +521,7 @@
 
     def decode_last():
         for f in range(direct, final + 1):
-            wait_recv(w_fine.at[0 : n_rep - 1, chunks[f]], w_rs.at[coarse + f])
+            wait_recv(w_fine.at[0 : n_rep - 1, chunks[f]], w_rs.at[ring(coarse + f)])
         wait_recv(w_fine.at[0:nc, shared_cols], v_rs.at[coarse])
         product = 0.0
         for owner in range(n_rep):
@@ -855,9 +861,9 @@
             dma((len(CHUNKS),)),
             dma((11,)),
             dma(()),
-            dma((units,)),
-            dma((units,)),
-            dma((units,)),
+            dma((RING + len(CHUNKS),)),
+            dma((RING + len(CHUNKS),)),
+            dma((RING + len(CHUNKS),)),
             dma((steps,)),
             dma(()),
         ],

time: 90.6 us -> 90.5 us (level)
  no operation moved by 1% of the time
where the time goes in v7:
time: 90.5 us; the launch traced here: 90.3 us
  Pallas kernels  89.7 us (99%)
    pallas_call x1, Pallas kernels, synchronise(): pl.pallas_call(functools.partial(sync_kernel, n_rep, n_tp, sub), out_shap...  87.7 us
    pallas_call x1, Pallas kernels, synchronise(): pl.pallas_call(finish_kernel, out_shape=[jax.ShapeDtypeStruct((rows, cols...  1.93 us

profile of v7, /device:TPU:0, one launch (start us, length us, event | category | flops | bytes accessed | tf_op | source)
XLA Modules:
  0.0 90.3 jit_solution(7033240073910848386)
XLA Ops:
  0.6 87.7 %synchronise.1 = (f32[256,1024]{1,0:T(8,128)S(1)}, f32[256,1024]{1,0:T(8,128)S(1)}, f32[256,1024]{1,0:T(8,128)S(1)}, f32[16,1024]{1,0:T(8,128)S(1)}, f32[16,1024...) custom-call(bf16[2048,2048]{1,0:T(8,128)(2,1)} %tok_hbm.1, ...), custom_call_target="tpu_custom_call" | custom-call | tf_op jit(solution)/shard_map/synchronise/pallas_call | solution.py:825
  88.4 1.9 %finish.1 = (f32[256,1024]{1,0:T(8,128)}, f32[256,1024]{1,0:T(8,128)}, f32[256,1024]{1,0:T(8,128)}, f32[16,1024]{1,0:T(8,128)}, f32[16,1024]{1,0:T(8,128)}, /*index=5*/f32[16,4096]{1,0:T(8,128)}, f32[16,4096]{1,0:T(8,128)}) custom-call(f32[256,1024]{1,0:T(8,128)S(1)} %get-tuple-element.24.master, f32[256,1024]{1,0:T(8,128)S(1)} %get-tuple-element.25.m1, ...), custom_call_target="tpu_custom_call" | custom-call | tf_op jit(solution)/shard_map/finish/pallas_call | solution.py:889
